TPU v7x, 32 devices: a whole 2x2x4 slice. The times are simulated.
32 devices in a mesh: segment: 4 (over y, x), dp: 8 (over z, core).
Axes of the slice: x: 2, y: 2, z: 4, core: 2. Of those that a mesh axis runs over, the one named last changes fastest.
Arguments:
- input_tiles: bfloat16 [16, 1024, 276], P('dp'), may hold values from -6 to 6
- truth_fields: bfloat16 [16, 1024, 276], P('dp'), may hold values from -6 to 6
- horizon_group_label: int32 [16], P('dp'), may hold values from 0 to 2
- var_ids: int32 [69], replicated, may hold values from 0 to 68
- spectral_basis: float32 [256, 256], replicated, may hold values from -0.375 to 0.375
- embed_rows: float32 [349, 384], P(None, 'dp'), may hold values from -6 to 6
- qkv_weight: float32 [2, 384, 1152], P(None, 'dp'), may hold values from -0.3125 to 0.3125
- out_weight: float32 [2, 384, 384], P(None, 'dp'), may hold values from -1.25 to 1.25
- up_weight: float32 [2, 384, 1536], P(None, 'dp'), may hold values from -0.3125 to 0.3125
- down_weight: float32 [2, 1536, 384], P(None, None, 'dp'), may hold values from -0.15625 to 0.15625
- ada_weight: float32 [2, 384, 2304], P(None, 'dp'), may hold values from -0.3125 to 0.3125
- head_weight: float32 [384, 276], P('dp'), may hold values from -0.3125 to 0.3125
- embed_momentum: float32 [349, 384], P(None, 'dp'), may hold values from -2.3841858e-06 to 2.3841858e-06
- qkv_momentum: float32 [2, 384, 1152], P(None, 'dp'), may hold values from -2.3841858e-06 to 2.3841858e-06
- out_momentum: float32 [2, 384, 384], P(None, 'dp'), may hold values from -2.3841858e-06 to 2.3841858e-06
- up_momentum: float32 [2, 384, 1536], P(None, 'dp'), may hold values from -2.3841858e-06 to 2.3841858e-06
- down_momentum: float32 [2, 1536, 384], P(None, None, 'dp'), may hold values from -2.3841858e-06 to 2.3841858e-06
- ada_momentum: float32 [2, 384, 2304], P(None, 'dp'), may hold values from -2.3841858e-06 to 2.3841858e-06
- head_momentum: float32 [384, 276], P('dp'), may hold values from -2.3841858e-06 to 2.3841858e-06
- embed_average: float32 [349, 384], P(None, 'dp'), may hold values from -6 to 6
- qkv_average: float32 [2, 384, 1152], P(None, 'dp'), may hold values from -0.3125 to 0.3125
- out_average: float32 [2, 384, 384], P(None, 'dp'), may hold values from -1.25 to 1.25
- up_average: float32 [2, 384, 1536], P(None, 'dp'), may hold values from -0.3125 to 0.3125
- down_average: float32 [2, 1536, 384], P(None, None, 'dp'), may hold values from -0.15625 to 0.15625
- ada_average: float32 [2, 384, 2304], P(None, 'dp'), may hold values from -0.3125 to 0.3125
- head_average: float32 [384, 276], P('dp'), may hold values from -0.3125 to 0.3125
Outputs:
- loss_value: float32 [], replicated
- clip_norm: float32 [], replicated
- embed_next: float32 [349, 384], P(None, 'dp')
- qkv_next: float32 [2, 384, 1152], P(None, 'dp')
- out_next: float32 [2, 384, 384], P(None, 'dp')
- up_next: float32 [2, 384, 1536], P(None, 'dp')
- down_next: float32 [2, 1536, 384], P(None, None, 'dp')
- ada_next: float32 [2, 384, 2304], P(None, 'dp')
- head_next: float32 [384, 276], P('dp')
- embed_momentum_next: float32 [349, 384], P(None, 'dp')
- qkv_momentum_next: float32 [2, 384, 1152], P(None, 'dp')
- out_momentum_next: float32 [2, 384, 384], P(None, 'dp')
- up_momentum_next: float32 [2, 384, 1536], P(None, 'dp')
- down_momentum_next: float32 [2, 1536, 384], P(None, None, 'dp')
- ada_momentum_next: float32 [2, 384, 2304], P(None, 'dp')
- head_momentum_next: float32 [384, 276], P('dp')
- embed_average_next: float32 [349, 384], P(None, 'dp')
- qkv_average_next: float32 [2, 384, 1152], P(None, 'dp')
- out_average_next: float32 [2, 384, 384], P(None, 'dp')
- up_average_next: float32 [2, 384, 1536], P(None, 'dp')
- down_average_next: float32 [2, 1536, 384], P(None, None, 'dp')
- ada_average_next: float32 [2, 384, 2304], P(None, 'dp')
- head_average_next: float32 [384, 276], P('dp')
Inputs may be any that keep to these rules, and one draw needn't show every extreme that they name: `horizon_group_label`: 0 stands for 6 h, 1 for 12 h, 2 for 24 h.
All inputs are finite; a program needn't handle non-finite values.
Results may differ from a plain program's by a relative error of at most 0.012.
The roundings to bfloat16 on the way count: a program that leaves them out, or rounds other values in their place, can miss the bound.
Values may be sent and summed in bfloat16 or wider, within the bound.
No kernel may reach another device: no remote copies, remote signals or barrier semaphores. Data moves between devices by JAX's collectives and lax.ppermute only.
A program may use at most 192 MiB of HBM per device.

v0:
```python
from functools import partial
import math

import jax
import jax.numpy as jnp
from jax import lax
from jax.sharding import PartitionSpec as P

D = 384
HEADS = 6
HEAD_DIM = 64
VARS = 69
CHANNELS = 69
LONP = 128
LATP = 8
LAYERS = 2
HORIZON_GROUPS = 3
QB = 512
TILE_FEATURES = 276


highest = lax.Precision.HIGHEST
eps_norm = 1e-06
clip_limit = 0.001
momentum_keep = 0.9
average_keep = 0.9
embed_boost = 20.0


def for_sending(x):

    def short(part):
        return part.astype(jnp.bfloat16) if part.dtype == jnp.float32 else part

    return jax.tree.map(short, x)


def passed_along(x, axis, by):
    length = lax.axis_size(axis)
    pairs = [(i, i + by) for i in range(length) if 0 <= i + by < length]
    return lax.ppermute(x, axis, pairs)


def matmul(left, right):
    return jnp.dot(left, right, precision=highest, preferred_element_type=jnp.float32)


def product(left, right):
    return jnp.dot(left, right, preferred_element_type=jnp.float32)


def product_back(left, right):
    return lax.dot_general(
        left, right, (((1,), (1,)), ((), ())), preferred_element_type=jnp.float32
    )


def product_outer(left, right):
    return lax.dot_general(
        left, right, (((0,), (0,)), ((), ())), preferred_element_type=jnp.float32
    )


def normalize(values):
    centered = values - jnp.mean(values, axis=-1, keepdims=True)
    return centered * lax.rsqrt(jnp.mean(centered * centered, axis=-1, keepdims=True) + eps_norm)


def modulate(values, offset, stretch):
    return normalize(values) * (1.0 + stretch) + offset


def aggregate(rows_float, grid_point_entries, var_ids):
    patch_rows = rows_float[:TILE_FEATURES]
    var_table = rows_float[TILE_FEATURES : TILE_FEATURES + VARS]
    agg_query = rows_float[TILE_FEATURES + VARS]
    one_hot = (var_ids[:, None] == jnp.arange(VARS, dtype=jnp.int32)[None, :]).astype(jnp.float32)
    channel_bases = matmul(one_hot, var_table)
    projected = matmul(patch_rows, agg_query[:, None])[:, 0].reshape(CHANNELS, 4)
    grouped = grid_point_entries.reshape(grid_point_entries.shape[0], CHANNELS, 4)
    scores = (
        jnp.sum(grouped * projected[None], axis=-1)
        + matmul(channel_bases, agg_query[:, None])[:, 0][None, :]
    )
    weights = jax.nn.softmax(scores * D ** (-0.5), axis=-1)
    spread = (weights[:, :, None] * grouped).reshape(grid_point_entries.shape[0], TILE_FEATURES)
    return (spread, matmul(weights, channel_bases))


def conditioning(ada_float, lead_rows, horizon_hours):
    one_hot = (jnp.arange(HORIZON_GROUPS, dtype=jnp.int32) == horizon_hours).astype(jnp.float32)
    condition = matmul(one_hot[None, :], lead_rows)[0]
    return matmul(jax.nn.silu(condition)[None, :], ada_float)[0].reshape(6, -1)


def split_heads(qkv_rows):
    return qkv_rows.reshape(qkv_rows.shape[0], 3, HEADS, HEAD_DIM).transpose(1, 2, 0, 3)


def head_blocks(heads_array, tokens):
    return heads_array.reshape(HEADS, tokens // QB, QB, HEAD_DIM).transpose(1, 0, 2, 3)


def spectrum(surface, spectral_basis):
    field_grid = surface.reshape(LATP, LONP, CHANNELS, 2, 2)
    wave_terms = jnp.einsum(
        "plcab,lbk->pcak", field_grid, spectral_basis.reshape(LONP, 2, 2 * LONP), precision=highest
    )
    return wave_terms[..., :LONP] ** 2 + wave_terms[..., LONP:] ** 2


def spread_layers(values, layer_index):
    return jnp.stack(
        [jnp.where(layer_index == position, values, 0.0) for position in range(LAYERS)]
    )


def attend(qkv_rows):
    tokens = qkv_rows.shape[0]
    sections = split_heads(qkv_rows)

    def one_block(query_block):
        scores = jnp.einsum(
            "hqd,hkd->hqk", query_block, sections[1], preferred_element_type=jnp.float32
        ) * HEAD_DIM ** (-0.5)
        row_top = jnp.max(scores, axis=-1, keepdims=True)
        exponent = jnp.exp(scores - row_top)
        row_total = jnp.sum(exponent, axis=-1, keepdims=True)
        probs = (exponent / row_total).astype(jnp.bfloat16)
        mixed = jnp.einsum("hqk,hkd->hqd", probs, sections[2], preferred_element_type=jnp.float32)
        return (mixed, row_top[..., 0] + jnp.log(row_total[..., 0]))

    outputs, log_sums = lax.map(one_block, head_blocks(sections[0], tokens))
    return (
        outputs.transpose(0, 2, 1, 3).reshape(tokens, HEADS * HEAD_DIM).astype(jnp.bfloat16),
        log_sums,
    )


def attend_back(qkv_rows, log_sums, grad_attended):
    tokens = qkv_rows.shape[0]
    sections = split_heads(qkv_rows)
    grad_heads = grad_attended.reshape(tokens, HEADS, HEAD_DIM).transpose(1, 0, 2)
    score_scale = HEAD_DIM ** (-0.5)

    def one_block(running_accumulator, inputs):
        query_block, grad_block, sum_block = inputs
        scores = (
            jnp.einsum("hqd,hkd->hqk", query_block, sections[1], preferred_element_type=jnp.float32)
            * score_scale
        )
        probs = jnp.exp(scores - sum_block[..., None])
        grad_probs = jnp.einsum(
            "hqd,hkd->hqk", grad_block, sections[2], preferred_element_type=jnp.float32
        )
        grad_scores = (
            probs * (grad_probs - jnp.sum(grad_probs * probs, axis=-1, keepdims=True))
        ).astype(jnp.bfloat16)
        grad_query = (
            jnp.einsum("hqk,hkd->hqd", grad_scores, sections[1], preferred_element_type=jnp.float32)
            * score_scale
        )
        grad_keys = (
            running_accumulator[0]
            + jnp.einsum(
                "hqk,hqd->hkd", grad_scores, query_block, preferred_element_type=jnp.float32
            )
            * score_scale
        )
        grad_values = running_accumulator[1] + jnp.einsum(
            "hqk,hqd->hkd",
            probs.astype(jnp.bfloat16),
            grad_block,
            preferred_element_type=jnp.float32,
        )
        return ((grad_keys, grad_values), grad_query)

    empty = jnp.zeros((HEADS, tokens, HEAD_DIM), jnp.float32)
    (grad_keys, grad_values), grad_queries = lax.scan(
        one_block,
        (empty, empty),
        (head_blocks(sections[0], tokens), head_blocks(grad_heads, tokens), log_sums),
    )
    grad_queries = grad_queries.transpose(1, 0, 2, 3).reshape(HEADS, tokens, HEAD_DIM)
    stacked = jnp.stack([grad_queries, grad_keys, grad_values])
    return stacked.transpose(2, 0, 1, 3).reshape(tokens, 3 * HEADS * HEAD_DIM).astype(jnp.bfloat16)


def block_forward(hidden, layer_weights, modulation):
    qkv_half, out_half, up_half, down_half = layer_weights
    normed = modulate(hidden, modulation[0], modulation[1]).astype(jnp.bfloat16)
    qkv_rows = product(normed, qkv_half).astype(jnp.bfloat16)
    attended, log_sums = attend(qkv_rows)
    branch_one = product(attended, out_half)
    middle = hidden + modulation[2] * branch_one
    normed_two = modulate(middle, modulation[3], modulation[4]).astype(jnp.bfloat16)
    hidden_units = product(normed_two, up_half)
    activated = jax.nn.gelu(hidden_units, approximate=True).astype(jnp.bfloat16)
    branch_two = product(activated, down_half)
    saved = (
        normed,
        qkv_rows,
        attended,
        log_sums,
        branch_one,
        middle,
        normed_two,
        hidden_units,
        activated,
        branch_two,
    )
    return (middle + modulation[5] * branch_two, saved)


def block_back(hidden, layer_weights, modulation, saved, grad_out):
    qkv_half, out_half, up_half, down_half = layer_weights
    (
        normed,
        qkv_rows,
        attended,
        log_sums,
        branch_one,
        middle,
        normed_two,
        hidden_units,
        activated,
        branch_two,
    ) = saved
    grad_two = (modulation[5] * grad_out).astype(jnp.bfloat16)
    grad_gate_two = jnp.sum(grad_out * branch_two, axis=0)
    grad_down = product_outer(activated, grad_two)
    unused, gelu_back = jax.vjp(partial(jax.nn.gelu, approximate=True), hidden_units)
    grad_units = gelu_back(product_back(grad_two, down_half))[0].astype(jnp.bfloat16)
    grad_up = product_outer(normed_two, grad_units)
    unused, second_back = jax.vjp(modulate, middle, modulation[3], modulation[4])
    grad_middle, grad_shift_two, grad_scale_two = second_back(product_back(grad_units, up_half))
    grad_middle = grad_middle + grad_out
    grad_one = (modulation[2] * grad_middle).astype(jnp.bfloat16)
    grad_gate_one = jnp.sum(grad_middle * branch_one, axis=0)
    grad_out_rows = product_outer(attended, grad_one)
    grad_rows = attend_back(
        qkv_rows, log_sums, product_back(grad_one, out_half).astype(jnp.bfloat16)
    )
    grad_qkv = product_outer(normed, grad_rows)
    unused, first_back = jax.vjp(modulate, hidden, modulation[0], modulation[1])
    grad_hidden, grad_shift_one, grad_scale_one = first_back(product_back(grad_rows, qkv_half))
    grad_modes = jnp.stack(
        [
            grad_shift_one,
            grad_scale_one,
            grad_gate_one,
            grad_shift_two,
            grad_scale_two,
            grad_gate_two,
        ]
    )
    return (grad_hidden + grad_middle, (grad_qkv, grad_out_rows, grad_up, grad_down), grad_modes)


def head_loss(hidden, head_half, truth_tile_matrix, spectral_basis):
    flat_rows = normalize(hidden).astype(jnp.bfloat16)
    predicted = product(flat_rows, head_half)
    power_gap = spectrum(predicted, spectral_basis) - spectrum(truth_tile_matrix, spectral_basis)
    return jnp.mean(power_gap * power_gap)


def per_device(
    input_tiles,
    truth_fields,
    horizon_group_label,
    var_ids,
    spectral_basis,
    embed_rows,
    qkv_weight,
    out_weight,
    up_weight,
    down_weight,
    ada_weight,
    head_weight,
    embed_momentum,
    qkv_momentum,
    out_momentum,
    up_momentum,
    down_momentum,
    ada_momentum,
    head_momentum,
    embed_average,
    qkv_average,
    out_average,
    up_average,
    down_average,
    ada_average,
    head_average,
):
    masters = (embed_rows, qkv_weight, out_weight, up_weight, down_weight, ada_weight, head_weight)
    moments = (
        embed_momentum,
        qkv_momentum,
        out_momentum,
        up_momentum,
        down_momentum,
        ada_momentum,
        head_momentum,
    )
    averages = (
        embed_average,
        qkv_average,
        out_average,
        up_average,
        down_average,
        ada_average,
        head_average,
    )
    rate_factors = (embed_boost, 1.0, 1.0, 1.0, 1.0, 1.0, 1.0)
    segment_count = lax.axis_size("segment")
    dp_count = lax.axis_size("dp")
    segment_index = lax.axis_index("segment")
    layer_index = jnp.clip(segment_index - 1, 0, LAYERS - 1)
    halves = tuple((weight.astype(jnp.bfloat16) for weight in masters))
    gathered = (
        lax.all_gather(halves[0], "dp", axis=1, tiled=True),
        lax.all_gather(halves[1], "dp", axis=1, tiled=True),
        lax.all_gather(halves[2], "dp", axis=1, tiled=True),
        lax.all_gather(halves[3], "dp", axis=1, tiled=True),
        lax.all_gather(halves[4], "dp", axis=2, tiled=True),
        lax.all_gather(halves[5], "dp", axis=1, tiled=True),
        lax.all_gather(halves[6], "dp", axis=0, tiled=True),
    )
    picked_layer = tuple(
        (
            lax.dynamic_index_in_dim(weight, layer_index, 0, keepdims=False)
            for weight in gathered[1:6]
        )
    )
    layer_weights = picked_layer[:4]
    ada_rows = picked_layer[4]
    rows_half = gathered[0]
    head_half = gathered[6]
    rows_float = rows_half.astype(jnp.float32)
    ada_float = ada_rows.astype(jnp.float32)
    lead_start = TILE_FEATURES + VARS + 1
    lead_float = rows_float[lead_start:]
    micro_count = input_tiles.shape[0]
    tokens = input_tiles.shape[1]
    segment_kind = jnp.where(
        segment_index == 0, 0, jnp.where(segment_index == segment_count - 1, 2, 1)
    )
    loss_seed = 1.0 / (micro_count * dp_count)
    zero_rows = jnp.zeros((tokens, D), jnp.bfloat16)
    zero_loss = jnp.zeros((), jnp.float32)

    def embed_forward(received, picked):
        spread, base_term = aggregate(rows_float, input_tiles[picked].astype(jnp.float32), var_ids)
        embedded = product(spread.astype(jnp.bfloat16), rows_half[:TILE_FEATURES]) + base_term
        return (embedded.astype(jnp.bfloat16), zero_loss)

    def block_segment_forward(received, picked):
        modulation = conditioning(ada_float, lead_float, horizon_group_label[picked])
        output, unused = block_forward(received.astype(jnp.float32), layer_weights, modulation)
        return (output.astype(jnp.bfloat16), zero_loss)

    def head_forward(received, picked):
        return (
            zero_rows,
            head_loss(
                received.astype(jnp.float32),
                head_half,
                truth_fields[picked].astype(jnp.float32),
                spectral_basis,
            ),
        )

    def spare_forward(received, picked):
        return (zero_rows, zero_loss)

    def forward_tick(tick_index, running_accumulator):
        stored, received, loss_sum = running_accumulator
        micro_index = tick_index - segment_index
        active = (micro_index >= 0) & (micro_index < micro_count)
        picked = jnp.clip(micro_index, 0, micro_count - 1)
        stored = jnp.where(
            active, lax.dynamic_update_index_in_dim(stored, received, picked, 0), stored
        )
        outgoing, part_loss = lax.switch(
            jnp.where(active, segment_kind, 3),
            (embed_forward, block_segment_forward, head_forward, spare_forward),
            received,
            picked,
        )
        received = jax.tree.map(
            lambda part, own: part.astype(own.dtype),
            passed_along(for_sending(outgoing), "segment", 1),
            outgoing,
        )
        return (stored, received, loss_sum + part_loss)

    stored, unused, loss_sum = lax.fori_loop(
        0,
        micro_count + segment_count - 1,
        forward_tick,
        (jnp.zeros((micro_count, tokens, D), jnp.bfloat16), zero_rows, zero_loss),
    )

    def embed_backward(received, picked, gradients):
        grid_point_entries = input_tiles[picked].astype(jnp.float32)

        def embed_part(rows_in):
            return aggregate(rows_in, grid_point_entries, var_ids)

        (spread, base_term), embed_back = jax.vjp(embed_part, rows_float)
        grad_patch = product_outer(spread.astype(jnp.bfloat16), received)
        grad_spread = product_back(received, rows_half[:TILE_FEATURES])
        grad_rows = embed_back((grad_spread, received.astype(jnp.float32)))[0]
        grad_rows = grad_rows + jnp.pad(
            grad_patch, ((0, grad_rows.shape[0] - TILE_FEATURES), (0, 0))
        )
        return (zero_rows, (gradients[0] + grad_rows,) + gradients[1:])

    def block_segment_backward(received, picked, gradients):
        hidden = stored[picked].astype(jnp.float32)

        def cond_part(ada_in, lead_in):
            return conditioning(ada_in, lead_in, horizon_group_label[picked])

        modulation, cond_back = jax.vjp(cond_part, ada_float, lead_float)
        output, saved = block_forward(hidden, layer_weights, modulation)
        grad_hidden, layer_grads, grad_modes = block_back(
            hidden, layer_weights, modulation, saved, received.astype(jnp.float32)
        )
        grad_ada, grad_lead = cond_back(grad_modes)
        grad_rows = jnp.pad(grad_lead, ((lead_start, 0), (0, 0)))
        updated = (
            gradients[0] + grad_rows,
            gradients[1] + layer_grads[0],
            gradients[2] + layer_grads[1],
            gradients[3] + layer_grads[2],
            gradients[4] + layer_grads[3],
            gradients[5] + grad_ada,
            gradients[6],
        )
        return (grad_hidden.astype(jnp.bfloat16), updated)

    def head_backward(received, picked, gradients):
        hidden = stored[picked].astype(jnp.float32)
        flat_rows, norm_back = jax.vjp(normalize, hidden)
        flat_half = flat_rows.astype(jnp.bfloat16)
        predicted = product(flat_half, head_half)
        target_power = spectrum(truth_fields[picked].astype(jnp.float32), spectral_basis)

        def power_loss(surface):
            power_gap = spectrum(surface, spectral_basis) - target_power
            return jnp.mean(power_gap * power_gap)

        unused_loss, loss_back = jax.vjp(power_loss, predicted)
        grad_pred = loss_back(jnp.full((), loss_seed, jnp.float32))[0].astype(jnp.bfloat16)
        grad_hidden = norm_back(product_back(grad_pred, head_half))[0]
        updated = gradients[:6] + (gradients[6] + product_outer(flat_half, grad_pred),)
        return (grad_hidden.astype(jnp.bfloat16), updated)

    def spare_backward(received, picked, gradients):
        return (zero_rows, gradients)

    def backward_tick(tick_index, running_accumulator):
        received, gradients = running_accumulator
        micro_index = tick_index - (segment_count - 1 - segment_index)
        active = (micro_index >= 0) & (micro_index < micro_count)
        picked = jnp.clip(micro_index, 0, micro_count - 1)
        outgoing, gradients = lax.switch(
            jnp.where(active, segment_kind, 3),
            (embed_backward, block_segment_backward, head_backward, spare_backward),
            received,
            picked,
            gradients,
        )
        received = jax.tree.map(
            lambda part, own: part.astype(own.dtype),
            passed_along(for_sending(outgoing), "segment", -1),
            outgoing,
        )
        return (received, gradients)

    starting = (
        (jnp.zeros(rows_half.shape, jnp.float32),)
        + tuple((jnp.zeros(weight.shape, jnp.float32) for weight in layer_weights))
        + (jnp.zeros(ada_rows.shape, jnp.float32), jnp.zeros(head_half.shape, jnp.float32))
    )
    unused, gradients = lax.fori_loop(
        0, micro_count + segment_count - 1, backward_tick, (zero_rows, starting)
    )
    stacked = tuple((spread_layers(part, layer_index) for part in gradients[1:6]))
    shards = (
        lax.psum_scatter(gradients[0], "dp", scatter_dimension=1, tiled=True),
        lax.psum_scatter(stacked[0], "dp", scatter_dimension=1, tiled=True),
        lax.psum_scatter(stacked[1], "dp", scatter_dimension=1, tiled=True),
        lax.psum_scatter(stacked[2], "dp", scatter_dimension=1, tiled=True),
        lax.psum_scatter(stacked[3], "dp", scatter_dimension=2, tiled=True),
        lax.psum_scatter(stacked[4], "dp", scatter_dimension=1, tiled=True),
        lax.psum_scatter(gradients[6], "dp", scatter_dimension=0, tiled=True),
    )
    accumulated_result = lax.psum(
        (shards[0], shards[1], shards[2], shards[3], shards[4], shards[5], shards[6], loss_sum),
        "segment",
    )
    local_squares = sum((jnp.sum(part * part) for part in accumulated_result[:7]))
    squares, loss_all = lax.psum((local_squares, accumulated_result[7]), "dp")
    loss_value = loss_all / (micro_count * dp_count)
    grad_norm = jnp.sqrt(squares)
    factor = clip_limit / jnp.maximum(grad_norm, clip_limit)
    params_count = sum((weight.size for weight in masters)) * dp_count
    step_rate = 0.02 * math.sqrt(params_count) / clip_limit
    new_weights, new_moments, new_averages = ([], [], [])
    for weight, moment, average, grad_part, rate_factor in zip(
        masters, moments, averages, accumulated_result[:7], rate_factors
    ):
        clipped = grad_part * factor
        moment_next = momentum_keep * moment + clipped
        weight_next = weight - step_rate * rate_factor * (clipped + momentum_keep * moment_next)
        new_weights.append(weight_next)
        new_moments.append(moment_next)
        new_averages.append(average_keep * average + (1.0 - average_keep) * weight_next)
    return (
        loss_value,
        grad_norm,
        new_weights[0],
        new_weights[1],
        new_weights[2],
        new_weights[3],
        new_weights[4],
        new_weights[5],
        new_weights[6],
        new_moments[0],
        new_moments[1],
        new_moments[2],
        new_moments[3],
        new_moments[4],
        new_moments[5],
        new_moments[6],
        new_averages[0],
        new_averages[1],
        new_averages[2],
        new_averages[3],
        new_averages[4],
        new_averages[5],
        new_averages[6],
    )


def solution(mesh):
    return jax.shard_map(
        per_device,
        mesh=mesh,
        in_specs=(
            P("dp", None, None),
            P("dp", None, None),
            P("dp"),
            P(),
            P(),
            P(None, "dp"),
            P(None, "dp", None),
            P(None, "dp", None),
            P(None, "dp", None),
            P(None, None, "dp"),
            P(None, "dp", None),
            P("dp", None),
            P(None, "dp"),
            P(None, "dp", None),
            P(None, "dp", None),
            P(None, "dp", None),
            P(None, None, "dp"),
            P(None, "dp", None),
            P("dp", None),
            P(None, "dp"),
            P(None, "dp", None),
            P(None, "dp", None),
            P(None, "dp", None),
            P(None, None, "dp"),
            P(None, "dp", None),
            P("dp", None),
        ),
        out_specs=(
            P(),
            P(),
            P(None, "dp"),
            P(None, "dp", None),
            P(None, "dp", None),
            P(None, "dp", None),
            P(None, None, "dp"),
            P(None, "dp", None),
            P("dp", None),
            P(None, "dp"),
            P(None, "dp", None),
            P(None, "dp", None),
            P(None, "dp", None),
            P(None, None, "dp"),
            P(None, "dp", None),
            P("dp", None),
            P(None, "dp"),
            P(None, "dp", None),
            P(None, "dp", None),
            P(None, "dp", None),
            P(None, None, "dp"),
            P(None, "dp", None),
            P("dp", None),
        ),
        check_vma=False,
    )
```

profile of v0, /device:TPU:0, one launch (start us, length us, event | category | flops | bytes accessed | tf_op | source)
XLA Modules:
  0.0 1670.4 jit_solution(4416438947014062511)
XLA Ops:
  80.2 31.3 %all-gather.9.cloned.1.call-done = bf16[2,384,1536]{2,1,0:T(8,128)(2,1)} async-done(((bf16[2,48,1536]{2,1,0:T(8,128)(2,1)}), bf16[2,384,1536]{2,1,0:T(8,128)(2,1)}) %all-gather.9.cloned.1.call-update) | async-done | bytes 2359312 | tf_op jit(solution)/shard_map/all_gather | solution.py:324
  113.9 40.3 %all-gather.5.cloned.1.call-done = bf16[2,384,2304]{2,1,0:T(8,128)(2,1)} async-done(((bf16[2,48,2304]{2,1,0:T(8,128)(2,1)}), bf16[2,384,2304]{2,1,0:T(8,128)(2,1)}) %all-gather.5.cloned.1.call-update) | async-done | bytes 3538960 | tf_op jit(solution)/shard_map/all_gather | solution.py:326
  159.2 331.1 %while.83 = (s32[]{:T(128)}, bf16[2,1024,384]{1,2,0:T(8,128)(2,1)}, bf16[1024,384]{0,1:T(8,128)(2,1)S(1)}, f32[]{:T(128)}, s32[]{:T(128)}, /*index=5*/s32[]{:T(1...) while((s32[]{:T(128)}, bf16[2,1024,384]{1,2,0:T(8,128)(2,1)}, ...), condition=%wide.region_19.20_spmd, body=%wide.region_0.19_spmd.sunk | while | flops 4481895424 | bytes 70146776 | solution.py:397
  178.4 21.4 %conditional.4 = (bf16[1024,384]{0,1:T(8,128)(2,1)}, f32[]{:T(128)}) conditional(s32[]{:T(128)} %clamp.18, (s32[]{:T(128)}, bf16[2,1024,276]{1,0,2:T(2,128)(2,1)}, f32[349,384]{1,0:T(8,128)}, s32[69]{0:T(128)}, bf16[349,384]{1,0:T(8,128)(2,1)}) %tuple.223, (bf16[1024,384]{0,1:T(8,128)(2,1)S(1)}, s32[]{:T(128)}, ...), branch_computations={%region_1.4_spmd, %region_5.13_spmd, %region_14.17_spmd, %region_1... | conditional | flops 4481502208 | bytes 63067872 | solution.py:384
  219.0 21.4 %conditional.4 = (bf16[1024,384]{0,1:T(8,128)(2,1)}, f32[]{:T(128)}) conditional(s32[]{:T(128)} %clamp.18, (s32[]{:T(128)}, bf16[2,1024,276]{1,0,2:T(2,128)(2,1)}, f32[349,384]{1,0:T(8,128)}, s32[69]{0:T(128)}, bf16[349,384]{1,0:T(8,128)(2,1)}) %tuple.223, (bf16[1024,384]{0,1:T(8,128)(2,1)S(1)}, s32[]{:T(128)}, ...), branch_computations={%region_1.4_spmd, %region_5.13_spmd, %region_14.17_spmd, %region_1... | conditional | flops 4481502208 | bytes 63067872 | solution.py:384
  240.4 46.1 %collective-permute-start.1 = (bf16[1024,384]{0,1:T(8,128)(2,1)}, bf16[1024,384]{0,1:T(8,128)(2,1)S(1)}, u32[]{:S(2)}, u32[]{:S(2)}) collective-permute-start(bf16[1024,384]{0,1:T(8,128)(2,1)} %get-tuple-element.2207), channel_id=1, source_target_pairs={{0,8},{8,16},{16,24},{1,9},{9,17},{17,25},{2,10},{10,18},{18,26},{... | collective-permute-start | bytes 2359304 | tf_op jit(solution)/shard_map/while/body/eval_jaxpr/ppermute | solution.py:41
  304.6 66.5 %collective-permute-start.1 = (bf16[1024,384]{0,1:T(8,128)(2,1)}, bf16[1024,384]{0,1:T(8,128)(2,1)S(1)}, u32[]{:S(2)}, u32[]{:S(2)}) collective-permute-start(bf16[1024,384]{0,1:T(8,128)(2,1)} %get-tuple-element.2207), channel_id=1, source_target_pairs={{0,8},{8,16},{16,24},{1,9},{9,17},{17,25},{2,10},{10,18},{18,26},{... | collective-permute-start | bytes 2359304 | tf_op jit(solution)/shard_map/while/body/eval_jaxpr/ppermute | solution.py:41
  408.8 66.9 %collective-permute-start.1 = (bf16[1024,384]{0,1:T(8,128)(2,1)}, bf16[1024,384]{0,1:T(8,128)(2,1)S(1)}, u32[]{:S(2)}, u32[]{:S(2)}) collective-permute-start(bf16[1024,384]{0,1:T(8,128)(2,1)} %get-tuple-element.2207), channel_id=1, source_target_pairs={{0,8},{8,16},{16,24},{1,9},{9,17},{17,25},{2,10},{10,18},{18,26},{... | collective-permute-start | bytes 2359304 | tf_op jit(solution)/shard_map/while/body/eval_jaxpr/ppermute | solution.py:41
  499.7 706.6 %while.84 = (s32[]{:T(128)}, bf16[1024,384]{0,1:T(8,128)(2,1)S(1)}, f32[349,384]{1,0:T(8,128)}, f32[384,1152]{1,0:T(8,128)}, f32[384,384]{1,0:T(8,128)}, /*index...) while((s32[]{:T(128)}, bf16[1024,384]{0,1:T(8,128)(2,1)S(1)}, ...), condition=%wide.region_59.60_spmd, body=%wide.region_22.59_spmd.sunk | while | flops 13884815360 | bytes 535473152 | solution.py:487
  505.9 17.4 %conditional.5 = (bf16[1024,384]{0,1:T(8,128)(2,1)}, f32[349,384]{1,0:T(8,128)}, f32[384,1152]{1,0:T(8,128)}, f32[384,384]{1,0:T(8,128)}, f32[384,1536]{1,0:T(8,...) conditional(s32[]{:T(128)} %clamp.19, (s32[69]{0:T(128)}, ...), branch_computations={%region_23.30_spmd, %region_31.52_spmd, %region_53.57_spmd, %regio... | conditional | flops 13884815360 | bytes 532326656 | solution.py:468
  524.6 18.2 %collective-permute-done = bf16[1024,384]{0,1:T(8,128)(2,1)S(1)} collective-permute-done((bf16[1024,384]{0,1:T(8,128)(2,1)}, bf16[1024,384]{0,1:T(8,128)(2,1)S(1)}, u32[]{:S(2)}, u32[]{:S(2)}) %collective-permute-start) | collective-permute-done | bytes 786464 | tf_op jit(solution)/shard_map/while/body/eval_jaxpr/ppermute | solution.py:41
  545.0 23.1 %collective-permute-done = bf16[1024,384]{0,1:T(8,128)(2,1)S(1)} collective-permute-done((bf16[1024,384]{0,1:T(8,128)(2,1)}, bf16[1024,384]{0,1:T(8,128)(2,1)S(1)}, u32[]{:S(2)}, u32[]{:S(2)}) %collective-permute-start) | collective-permute-done | bytes 786464 | tf_op jit(solution)/shard_map/while/body/eval_jaxpr/ppermute | solution.py:41
  570.3 375.9 %collective-permute-done = bf16[1024,384]{0,1:T(8,128)(2,1)S(1)} collective-permute-done((bf16[1024,384]{0,1:T(8,128)(2,1)}, bf16[1024,384]{0,1:T(8,128)(2,1)S(1)}, u32[]{:S(2)}, u32[]{:S(2)}) %collective-permute-start) | collective-permute-done | bytes 786464 | tf_op jit(solution)/shard_map/while/body/eval_jaxpr/ppermute | solution.py:41
  946.3 30.3 %conditional.5 = (bf16[1024,384]{0,1:T(8,128)(2,1)}, f32[349,384]{1,0:T(8,128)}, f32[384,1152]{1,0:T(8,128)}, f32[384,384]{1,0:T(8,128)}, f32[384,1536]{1,0:T(8,...) conditional(s32[]{:T(128)} %clamp.19, (s32[69]{0:T(128)}, ...), branch_computations={%region_23.30_spmd, %region_31.52_spmd, %region_53.57_spmd, %regio... | conditional | flops 13884815360 | bytes 532326656 | solution.py:468
  977.9 178.6 %collective-permute-done = bf16[1024,384]{0,1:T(8,128)(2,1)S(1)} collective-permute-done((bf16[1024,384]{0,1:T(8,128)(2,1)}, bf16[1024,384]{0,1:T(8,128)(2,1)S(1)}, u32[]{:S(2)}, u32[]{:S(2)}) %collective-permute-start) | collective-permute-done | bytes 786464 | tf_op jit(solution)/shard_map/while/body/eval_jaxpr/ppermute | solution.py:41
  1156.5 29.2 %conditional.5 = (bf16[1024,384]{0,1:T(8,128)(2,1)}, f32[349,384]{1,0:T(8,128)}, f32[384,1152]{1,0:T(8,128)}, f32[384,384]{1,0:T(8,128)}, f32[384,1536]{1,0:T(8,...) conditional(s32[]{:T(128)} %clamp.19, (s32[69]{0:T(128)}, ...), branch_computations={%region_23.30_spmd, %region_31.52_spmd, %region_53.57_spmd, %regio... | conditional | flops 13884815360 | bytes 532326656 | solution.py:468
  1237.1 32.9 %reduce-scatter.12.cloned.1.call-done = f32[2,48,384]{2,1,0:T(8,128)} async-done(((f32[2,384,384]{2,1,0:T(8,128)}), f32[2,48,384]{2,1,0:T(8,128)}) %reduce-scatter.12.cloned.1.call-update) | async-done | bytes 147472 | tf_op jit(solution)/shard_map/reduce_scatter | solution.py:494
  1269.9 44.4 %reduce-scatter.10.cloned.1.call-done = f32[2,48,1152]{2,1,0:T(8,128)} async-done(((f32[2,384,1152]{2,1,0:T(8,128)}), f32[2,48,1152]{2,1,0:T(8,128)}) %reduce-scatter.10.cloned.1.call-update) | async-done | bytes 442384 | tf_op jit(solution)/shard_map/reduce_scatter | solution.py:493
  1314.4 55.9 %reduce-scatter.16.cloned.1.call-done = f32[2,1536,48]{1,2,0:T(8,128)} async-done(((f32[2,1536,384]{1,2,0:T(8,128)}), f32[2,1536,48]{1,2,0:T(8,128)}) %reduce-scatter.16.cloned.1.call-update) | async-done | bytes 589840 | tf_op jit(solution)/shard_map/reduce_scatter | solution.py:496
  1370.3 55.8 %reduce-scatter.14.cloned.1.call-done = f32[2,48,1536]{2,1,0:T(8,128)} async-done(((f32[2,384,1536]{2,1,0:T(8,128)}), f32[2,48,1536]{2,1,0:T(8,128)}) %reduce-scatter.14.cloned.1.call-update) | async-done | bytes 589840 | tf_op jit(solution)/shard_map/reduce_scatter | solution.py:495
  1426.0 77.9 %reduce-scatter.18.cloned.1.call-done = f32[2,48,2304]{2,1,0:T(8,128)} async-done(((f32[2,384,2304]{2,1,0:T(8,128)}), f32[2,48,2304]{2,1,0:T(8,128)}) %reduce-scatter.18.cloned.1.call-update) | async-done | bytes 884752 | tf_op jit(solution)/shard_map/reduce_scatter | solution.py:497
  1504.0 32.5 %reduce-scatter.20.cloned.1.call-done = f32[48,276]{1,0:T(8,128)} async-done(((f32[384,276]{1,0:T(8,128)}), f32[48,276]{1,0:T(8,128)}) %reduce-scatter.20.cloned.1.call-update) | async-done | bytes 53008 | tf_op jit(solution)/shard_map/reduce_scatter | solution.py:498
  1536.5 19.9 %all-reduce.8 = (f32[]{:T(128)}, f32[48,276]{1,0:T(8,128)S(1)}) all-reduce(f32[]{:T(128)} %get-tuple-element.1254, f32[48,276]{1,0:T(8,128)} %reduce-scatter.20.cloned.1.call-done), channel_id=1, replica_groups=mesh['segment'=4,'dp'=8] {'segment'}, use_global_device_ids=true, to_apply=%region_20.21 | all-reduce | flops 13249 | bytes 105992 | tf_op jit(solution)/shard_map/psum | solution.py:500
  1556.9 63.7 %all-reduce.12.cloned.1.call-done = (f32[349,48]{0,1:T(8,128)}, f32[2,48,1152]{2,1,0:T(8,128)}, f32[2,48,384]{2,1,0:T(8,128)}, f32[2,48,1536]{2,1,0:T(8,128)}, f...) async-done(((f32[349,48]{0,1:T(8,128)}, f32[2,48,1152]{2,1,0:T(8,128)}, f32[2,48,384]{2,1,0:T(8,128)}, f32[2,48,1536]{2,1,0:T(8,128)}, f32[2,1536,48]{1,2,0:T(8,128)}, ...) | async-done | bytes 2721232 | tf_op jit(solution)/shard_map/psum | solution.py:500
  (320 shorter events, 373.7 us)
Async XLA Ops:
  7.2 58.1 %all-gather.7.cloned.1.call-start = ((), (), s32[]{:S(2)}) async-start(), calls=%async_computation.8 | async-start | bytes 1990656 | tf_op jit(solution)/shard_map/all_gather | solution.py:322
  9.1 68.3 %all-gather.11.cloned.1.call-start = ((), (), s32[]{:S(2)}) async-start(), calls=%async_computation.10 | async-start | bytes 2654208 | tf_op jit(solution)/shard_map/all_gather | solution.py:325
  11.0 100.5 %all-gather.9.cloned.1.call-start = ((), (), s32[]{:S(2)}) async-start(), calls=%async_computation.9 | async-start | bytes 2654208 | tf_op jit(solution)/shard_map/all_gather | solution.py:324
  11.8 142.4 %all-gather.5.cloned.1.call-start = ((), (), s32[]{:S(2)}) async-start(), calls=%async_computation.7 | async-start | bytes 3981312 | tf_op jit(solution)/shard_map/all_gather | solution.py:326
  12.7 1224.3 %reduce-scatter.8.cloned.1.call-start = ((), (), s32[]{:S(2)}) async-start(), calls=%async_computation.11 | async-start | bytes 663552 | tf_op jit(solution)/shard_map/reduce_scatter | solution.py:492
  199.8 19.1 %collective-permute-start.1 = (bf16[1024,384]{0,1:T(8,128)(2,1)}, bf16[1024,384]{0,1:T(8,128)(2,1)S(1)}, u32[]{:S(2)}, u32[]{:S(2)}) collective-permute-start(bf16[1024,384]{0,1:T(8,128)(2,1)} %get-tuple-element.2207), channel_id=1, source_target_pairs={{0,8},{8,16},{16,24},{1,9},{9,17},{17,25},{2,10},{10,18},{18,26},{... | collective-permute-start | bytes 2359304 | tf_op jit(solution)/shard_map/while/body/eval_jaxpr/ppermute | solution.py:41
  240.4 63.0 %collective-permute-start.1 = (bf16[1024,384]{0,1:T(8,128)(2,1)}, bf16[1024,384]{0,1:T(8,128)(2,1)S(1)}, u32[]{:S(2)}, u32[]{:S(2)}) collective-permute-start(bf16[1024,384]{0,1:T(8,128)(2,1)} %get-tuple-element.2207), channel_id=1, source_target_pairs={{0,8},{8,16},{16,24},{1,9},{9,17},{17,25},{2,10},{10,18},{18,26},{... | collective-permute-start | bytes 2359304 | tf_op jit(solution)/shard_map/while/body/eval_jaxpr/ppermute | solution.py:41
  304.6 82.6 %collective-permute-start.1 = (bf16[1024,384]{0,1:T(8,128)(2,1)}, bf16[1024,384]{0,1:T(8,128)(2,1)S(1)}, u32[]{:S(2)}, u32[]{:S(2)}) collective-permute-start(bf16[1024,384]{0,1:T(8,128)(2,1)} %get-tuple-element.2207), channel_id=1, source_target_pairs={{0,8},{8,16},{16,24},{1,9},{9,17},{17,25},{2,10},{10,18},{18,26},{... | collective-permute-start | bytes 2359304 | tf_op jit(solution)/shard_map/while/body/eval_jaxpr/ppermute | solution.py:41
  388.2 19.5 %collective-permute-start.1 = (bf16[1024,384]{0,1:T(8,128)(2,1)}, bf16[1024,384]{0,1:T(8,128)(2,1)S(1)}, u32[]{:S(2)}, u32[]{:S(2)}) collective-permute-start(bf16[1024,384]{0,1:T(8,128)(2,1)} %get-tuple-element.2207), channel_id=1, source_target_pairs={{0,8},{8,16},{16,24},{1,9},{9,17},{17,25},{2,10},{10,18},{18,26},{... | collective-permute-start | bytes 2359304 | tf_op jit(solution)/shard_map/while/body/eval_jaxpr/ppermute | solution.py:41
  408.8 81.4 %collective-permute-start.1 = (bf16[1024,384]{0,1:T(8,128)(2,1)}, bf16[1024,384]{0,1:T(8,128)(2,1)S(1)}, u32[]{:S(2)}, u32[]{:S(2)}) collective-permute-start(bf16[1024,384]{0,1:T(8,128)(2,1)} %get-tuple-element.2207), channel_id=1, source_target_pairs={{0,8},{8,16},{16,24},{1,9},{9,17},{17,25},{2,10},{10,18},{18,26},{... | collective-permute-start | bytes 2359304 | tf_op jit(solution)/shard_map/while/body/eval_jaxpr/ppermute | solution.py:41
  523.3 19.5 %collective-permute-start = (bf16[1024,384]{0,1:T(8,128)(2,1)}, bf16[1024,384]{0,1:T(8,128)(2,1)S(1)}, u32[]{:S(2)}, u32[]{:S(2)}) collective-permute-start(bf16[1024,384]{0,1:T(8,128)(2,1)} %get-tuple-element.2235), channel_id=1, source_target_pairs={{8,0},{16,8},{24,16},{9,1},{17,9},{25,17},{10,2},{18,10},{26,18},{... | collective-permute-start | bytes 2359304 | tf_op jit(solution)/shard_map/while/body/eval_jaxpr/ppermute | solution.py:41
  543.7 24.3 %collective-permute-start = (bf16[1024,384]{0,1:T(8,128)(2,1)}, bf16[1024,384]{0,1:T(8,128)(2,1)S(1)}, u32[]{:S(2)}, u32[]{:S(2)}) collective-permute-start(bf16[1024,384]{0,1:T(8,128)(2,1)} %get-tuple-element.2235), channel_id=1, source_target_pairs={{8,0},{16,8},{24,16},{9,1},{17,9},{25,17},{10,2},{18,10},{26,18},{... | collective-permute-start | bytes 2359304 | tf_op jit(solution)/shard_map/while/body/eval_jaxpr/ppermute | solution.py:41
  569.1 377.2 %collective-permute-start = (bf16[1024,384]{0,1:T(8,128)(2,1)}, bf16[1024,384]{0,1:T(8,128)(2,1)S(1)}, u32[]{:S(2)}, u32[]{:S(2)}) collective-permute-start(bf16[1024,384]{0,1:T(8,128)(2,1)} %get-tuple-element.2235), channel_id=1, source_target_pairs={{8,0},{16,8},{24,16},{9,1},{17,9},{25,17},{10,2},{18,10},{26,18},{... | collective-permute-start | bytes 2359304 | tf_op jit(solution)/shard_map/while/body/eval_jaxpr/ppermute | solution.py:41
  976.6 179.9 %collective-permute-start = (bf16[1024,384]{0,1:T(8,128)(2,1)}, bf16[1024,384]{0,1:T(8,128)(2,1)S(1)}, u32[]{:S(2)}, u32[]{:S(2)}) collective-permute-start(bf16[1024,384]{0,1:T(8,128)(2,1)} %get-tuple-element.2235), channel_id=1, source_target_pairs={{8,0},{16,8},{24,16},{9,1},{17,9},{25,17},{10,2},{18,10},{26,18},{... | collective-permute-start | bytes 2359304 | tf_op jit(solution)/shard_map/while/body/eval_jaxpr/ppermute | solution.py:41
  1185.7 15.4 collective-permute-start
  1208.5 61.4 %reduce-scatter.12.cloned.1.call-start = ((), (), s32[]{:S(2)}) async-start(), calls=%async_computation.13 | async-start | bytes 1327104 | tf_op jit(solution)/shard_map/reduce_scatter | solution.py:494
  1209.8 104.5 %reduce-scatter.10.cloned.1.call-start = ((), (), s32[]{:S(2)}) async-start(), calls=%async_computation.12 | async-start | bytes 3981312 | tf_op jit(solution)/shard_map/reduce_scatter | solution.py:493
  1212.9 157.4 %reduce-scatter.16.cloned.1.call-start = ((), (), s32[]{:S(2)}) async-start(), calls=%async_computation.15 | async-start | bytes 5308416 | tf_op jit(solution)/shard_map/reduce_scatter | solution.py:496
  1221.2 204.8 %reduce-scatter.14.cloned.1.call-start = ((), (), s32[]{:S(2)}) async-start(), calls=%async_computation.14 | async-start | bytes 5308416 | tf_op jit(solution)/shard_map/reduce_scatter | solution.py:495
  1226.0 278.0 %reduce-scatter.18.cloned.1.call-start = ((), (), s32[]{:S(2)}) async-start(), calls=%async_computation.16 | async-start | bytes 7962624 | tf_op jit(solution)/shard_map/reduce_scatter | solution.py:497
  1231.8 304.7 %reduce-scatter.20.cloned.1.call-start = ((), (), s32[]{:S(2)}) async-start(), calls=%async_computation.17 | async-start | bytes 663552 | tf_op jit(solution)/shard_map/reduce_scatter | solution.py:498
  1232.5 388.1 %all-reduce.12.cloned.1.call-start = ((), (), s32[]{:S(2)}) async-start(), calls=%async_computation.18 | async-start | bytes 5455872 | tf_op jit(solution)/shard_map/psum | solution.py:500
  1504.0 146.4 %copy-start.90 = (f32[349,48]{0,1:T(8,128)S(1)}, f32[349,48]{0,1:T(8,128)}, u32[]{:S(2)}) copy-start(f32[349,48]{0,1:T(8,128)} %param.49) | copy-start | bytes 201028
  1504.0 146.4 %copy-start.99 = (f32[349,48]{0,1:T(8,128)S(1)}, f32[349,48]{0,1:T(8,128)}, u32[]{:S(2)}) copy-start(f32[349,48]{0,1:T(8,128)} %param.63) | copy-start | bytes 201028
  (46 other events, 523.1 us)
Sparse Core Ops, SparseCore 0:
  10.2 31.0 all-gather.6
  43.5 33.9 all-gather.10
  79.6 31.8 all-gather.8
  113.5 40.6 all-gather.4
  1208.6 28.3 reduce-scatter.7
  1239.2 30.6 reduce-scatter.11
  1272.3 42.0 reduce-scatter.9
  1316.8 53.4 reduce-scatter.15
  1372.7 53.3 reduce-scatter.13
  1428.3 75.5 reduce-scatter.17
  1506.9 29.5 reduce-scatter.19
  1540.6 79.9 all-reduce.11
where the time goes:
time: 1680 us; the launch traced here: 1670 us
  waiting for transfers between devices  1130 us (67%)
  starting transfers between devices  192 us (11%)
  local copies, waits for them, and re-layouts  88.7 us (5%)
  blocking collectives  85.9 us (5%)
  other arithmetic  66.1 us (4%)
  loops' own time  49.1 us (3%)
  matrix products  37.2 us (2%)
  between operations  22.9 us (1%)
    ppermute x10, waiting for transfers between devices, passed_along(): return lax.ppermute(x, axis, pairs)  679 us
    ppermute x10, starting transfers between devices, passed_along(): return lax.ppermute(x, axis, pairs)  191 us
    reduce_scatter x1, waiting for transfers between devices, per_device(): lax.psum_scatter(stacked[4], 'dp', scatter_dimension=1, tiled=True)  77.9 us
    psum x1, waiting for transfers between devices, per_device(): lax.psum((shards[0], shards[1], shards[2], shards[3], shards[4], shards[5...  63.7 us
    reduce_scatter x1, waiting for transfers between devices, per_device(): lax.psum_scatter(stacked[3], 'dp', scatter_dimension=2, tiled=True)  55.9 us
    reduce_scatter x1, waiting for transfers between devices, per_device(): lax.psum_scatter(stacked[2], 'dp', scatter_dimension=1, tiled=True)  55.8 us
    reduce_scatter x1, waiting for transfers between devices, per_device(): lax.psum_scatter(stacked[0], 'dp', scatter_dimension=1, tiled=True)  44.4 us
    all_gather x1, waiting for transfers between devices, per_device(): lax.all_gather(halves[5], 'dp', axis=1, tiled=True)  40.3 us
  transfers between devices with their start and end apart: 22, of which 21 were waited for; matrix products, arithmetic and copies ran while one was open for 3% of the time, Pallas kernels for 0%

commit v1 on v0

v1 whole, which is shorter than its diff:
```python
import math

import jax
import jax.numpy as jnp
from jax import lax
from jax.experimental import pallas as pl
from jax.experimental.pallas import tpu as pltpu
from jax.sharding import Mesh, PartitionSpec as P

D = 384
HEADS = 6
HEAD_DIM = 64
FF = 1536
VARS = 69
CHANNELS = 69
LONP = 128
LATP = 8
LAYERS = 2
GROUPS = 3
PIXELS = 276
LEAD = PIXELS + VARS + 1
EROWS = LEAD + GROUPS
ECOLS = 512
EPS = 1e-06
CLIP = 0.001
KEEP = 0.9
BOOST = 20.0
LABEL_LANE = D - 1
HALF = FF // 2

F32 = jnp.float32
BF16 = jnp.bfloat16
CHIP = ("s", "z", "c")


def dot(a, b):
    return jnp.dot(a, b, preferred_element_type=F32)


def dot_nt(a, b):
    return lax.dot_general(a, b, (((1,), (1,)), ((), ())), preferred_element_type=F32)


def dot_tn(a, b):
    return lax.dot_general(a, b, (((0,), (0,)), ((), ())), preferred_element_type=F32)


def parts(x, count):
    out = []
    for step in range(count):
        piece = x.astype(BF16)
        out.append(piece)
        if step < count - 1:
            x = x - piece.astype(F32)
    return out


def normal(v):
    centered = v - jnp.mean(v, axis=-1, keepdims=True)
    inverse = lax.rsqrt(jnp.mean(centered * centered, axis=-1, keepdims=True) + EPS)
    return centered * inverse, inverse


def normal_back(d_x, x, inverse):
    return inverse * (
        d_x - jnp.mean(d_x, axis=-1, keepdims=True) - x * jnp.mean(d_x * x, axis=-1, keepdims=True)
    )


def lane_below(limit, shape):
    return lax.broadcasted_iota(jnp.int32, shape, len(shape) - 1) < limit


def same_group():
    row = lax.broadcasted_iota(jnp.int32, (D, D), 0)
    col = lax.broadcasted_iota(jnp.int32, (D, D), 1)
    return (row // 4 == col // 4).astype(BF16)


def chosen_table(vid_ref):
    row = lax.broadcasted_iota(jnp.int32, (ECOLS, D), 0)
    return (row - PIXELS == vid_ref[...]).astype(BF16)


def first_of_four(shape):
    lane = lax.broadcasted_iota(jnp.int32, shape, len(shape) - 1)
    return lane % 4 == 0


def cost(flops, size, exps=0):
    return pl.CostEstimate(flops=int(flops), bytes_accessed=int(size), transcendentals=int(exps))


def params(limit=40):
    return pltpu.CompilerParams(vmem_limit_bytes=limit << 20)


def embed_kernel(tiles_ref, emb_ref, vid_ref, out_ref, agg_ref, row_sc, base_sc, bases_sc):
    @pl.when(pl.program_id(0) == 0)
    def _():
        emb = emb_ref[...].astype(F32)
        row = jnp.sum(emb * emb[:, LEAD - 1 : LEAD], axis=0, keepdims=True)
        row_sc[...] = jnp.where(lane_below(PIXELS, (1, D)), row[:, :D], 0.0)
        table = chosen_table(vid_ref)
        wide = jnp.broadcast_to(row, (8, ECOLS))
        base_sc[...] = sum(dot(p, table) for p in parts(wide, 3))[:1]
        bases = dot(emb_ref[...], table)
        bases_sc[...] = jnp.where(first_of_four((D, D)), bases, 0.0).astype(BF16)

    x = tiles_ref[...].astype(F32)
    group = same_group()
    scores = sum(dot(p, group) for p in parts(x * row_sc[...], 3)) + base_sc[...]
    scores = jnp.where(lane_below(PIXELS, scores.shape), scores * D ** (-0.5), -1e30)
    e = jnp.exp(scores - jnp.max(scores, axis=-1, keepdims=True))
    agg = e / (0.25 * jnp.sum(e, axis=-1, keepdims=True))
    agg_ref[...] = agg
    spread = (agg * x).astype(BF16)
    total = dot_nt(spread, emb_ref[:, :D])
    for p in parts(agg, 2):
        total = total + dot_nt(p, bases_sc[...])
    out_ref[...] = total.astype(BF16)


def embed(data, emb, vid4, tokens):
    rows = 256
    return pl.pallas_call(
        embed_kernel,
        grid=(tokens // rows,),
        in_specs=[
            pl.BlockSpec((rows, D), lambda i: (i, 0)),
            pl.BlockSpec((D, ECOLS), lambda i: (0, 0)),
            pl.BlockSpec((1, D), lambda i: (0, 0)),
        ],
        out_specs=[
            pl.BlockSpec((rows, D), lambda i: (i, 0)),
            pl.BlockSpec((rows, D), lambda i: (i, 0)),
        ],
        out_shape=[
            jax.ShapeDtypeStruct((tokens, D), BF16),
            jax.ShapeDtypeStruct((tokens, D), F32),
        ],
        scratch_shapes=[
            pltpu.VMEM((1, D), F32),
            pltpu.VMEM((1, D), F32),
            pltpu.VMEM((D, D), BF16),
        ],
        compiler_params=params(),
        cost_estimate=cost(2e9 * 3, 4e6, 4e5),
        name="embed",
    )(data, emb, vid4)


def embed_back_kernel(dh_ref, tiles_ref, agg_ref, emb_ref, vid_ref, out_ref):
    dh = dh_ref[...]
    x = tiles_ref[...].astype(F32)
    agg = agg_ref[...]
    emb = emb_ref[...]
    table = chosen_table(vid_ref)
    group = same_group()
    bases = dot(emb, table).astype(BF16)
    query = emb[:, LEAD - 1 : LEAD].astype(F32)
    spread = (agg * x).astype(BF16)
    g_patch = dot_tn(dh, spread)
    d_spread = dot(dh, emb[:, :D])
    d_agg = dot(dh, bases)
    for p in parts(d_spread * x, 2):
        d_agg = d_agg + dot(p, group)
    inner = 0.25 * jnp.sum(agg * d_agg, axis=-1, keepdims=True)
    d_scores = agg * (d_agg - inner) * D ** (-0.5)
    d_proj = jnp.sum(d_scores * x, axis=0, keepdims=True)
    d_base = jnp.sum(d_scores, axis=0, keepdims=True)
    d_base = jnp.where(first_of_four(d_base.shape), d_base, 0.0)
    only = first_of_four(agg.shape)
    d_bases = query * d_base
    for p in parts(jnp.where(only, agg, 0.0), 2):
        d_bases = d_bases + dot_tn(dh, p)
    g_table = sum(dot_nt(p, table) for p in parts(d_bases, 2))
    d_query = jnp.sum(
        emb[:, :D].astype(F32) * d_proj + bases.astype(F32) * d_base, axis=-1, keepdims=True
    )
    lane = lax.broadcasted_iota(jnp.int32, (D, ECOLS), 1)
    total = g_table + jnp.where(lane == LEAD - 1, d_query, 0.0)
    first = total[:, :D] + g_patch + query * d_proj
    for j in range(3):
        out_ref[j] = first[:, 128 * j : 128 * j + 128].astype(BF16)
    out_ref[3] = total[:, D:].astype(BF16)


def embed_back(dh, data, agg, emb, vid4):
    rows = dh.shape[0]
    return pl.pallas_call(
        embed_back_kernel,
        grid=(1,),
        in_specs=[
            pl.BlockSpec((rows, D), lambda i: (0, 0)),
            pl.BlockSpec((rows, D), lambda i: (0, 0)),
            pl.BlockSpec((rows, D), lambda i: (0, 0)),
            pl.BlockSpec((D, ECOLS), lambda i: (0, 0)),
            pl.BlockSpec((1, D), lambda i: (0, 0)),
        ],
        out_specs=pl.BlockSpec((4, D, 128), lambda i: (0, 0, 0)),
        out_shape=jax.ShapeDtypeStruct((4, D, 128), BF16),
        compiler_params=params(),
        cost_estimate=cost(3e9, 4e6),
        name="embed_back",
    )(dh, data, agg, emb, vid4)


def qkv_kernel(h_ref, mod_ref, w_ref, normed_ref, qkv_ref):
    x, _ = normal(h_ref[...].astype(F32))
    normed = (x * (1.0 + mod_ref[1:2]) + mod_ref[0:1]).astype(BF16)
    normed_ref[...] = normed
    for j in range(3):
        qkv_ref[:, D * j : D * (j + 1)] = dot(normed, w_ref[j]).astype(BF16)


def qkv_rows(h, start, count, mod, weights):
    rows = 256
    return pl.pallas_call(
        qkv_kernel,
        grid=(count // rows,),
        in_specs=[
            pl.BlockSpec((rows, D), lambda i: (i + start // rows, 0)),
            pl.BlockSpec((8, D), lambda i: (0, 0)),
            pl.BlockSpec((4, D, D), lambda i: (0, 0, 0)),
        ],
        out_specs=[
            pl.BlockSpec((rows, D), lambda i: (i, 0)),
            pl.BlockSpec((rows, 3 * D), lambda i: (i, 0)),
        ],
        out_shape=[
            jax.ShapeDtypeStruct((count, D), BF16),
            jax.ShapeDtypeStruct((count, 3 * D), BF16),
        ],
        compiler_params=params(),
        cost_estimate=cost(2 * count * D * 3 * D, 3e6),
        name="qkv_rows",
    )(h, mod, weights)


def pair_masks():
    low = lane_below(HEAD_DIM, (1, 128))
    return low, jnp.logical_not(low)


def block_kernel(
    h_ref,
    q_ref,
    own_ref,
    other_ref,
    mod_ref,
    w_ref,
    out_ref,
    att_ref,
    lse_ref,
    one_ref,
    mid_ref,
    n2_ref,
    units_ref,
    act_ref,
    two_ref,
):
    zero = jnp.zeros((), BF16)
    rows = h_ref.shape[0]
    lane = lax.broadcasted_iota(jnp.int32, (rows, 128), 1)
    sums = jnp.zeros((rows, 128), F32)
    attended = []
    for pair in range(HEADS // 2):
        a = 128 * pair
        q = q_ref[:, a : a + 128] * 0.125
        keys = jnp.concatenate([own_ref[:, D + a : D + a + 128], other_ref[:, D + a : D + a + 128]])
        vals = jnp.concatenate(
            [own_ref[:, 2 * D + a : 2 * D + a + 128], other_ref[:, 2 * D + a : 2 * D + a + 128]]
        )
        mixed = jnp.zeros((rows, 128), F32)
        for which, mask in enumerate(pair_masks()):
            scores = dot_nt(q, jnp.where(mask, keys, zero))
            top = jnp.max(scores, axis=-1, keepdims=True)
            e = jnp.exp(scores - top)
            total = jnp.sum(e, axis=-1, keepdims=True)
            probs = (e * (1.0 / total)).astype(BF16)
            mixed = mixed + dot(probs, jnp.where(mask, vals, zero))
            sums = jnp.where(lane == 2 * pair + which, top + jnp.log(total), sums)
        attended.append(mixed.astype(BF16))
    lse_ref[...] = sums
    attended = jnp.concatenate(attended, axis=-1)
    att_ref[...] = attended
    one = dot(attended, w_ref[3, :, :D])
    one_ref[...] = one
    middle = h_ref[...].astype(F32) + mod_ref[2:3] * one
    mid_ref[...] = middle
    x, _ = normal(middle)
    n2 = (x * (1.0 + mod_ref[4:5]) + mod_ref[3:4]).astype(BF16)
    n2_ref[...] = n2
    two = jnp.zeros((rows, D), F32)
    for j in range(2):
        units = dot(n2, w_ref[j, :, D:])
        units_ref[:, HALF * j : HALF * (j + 1)] = units
        act = jax.nn.gelu(units, approximate=True).astype(BF16)
        act_ref[:, HALF * j : HALF * (j + 1)] = act
        two = two + dot_nt(act, w_ref[2 + j, :, D:])
    two_ref[...] = two
    out_ref[...] = (middle + mod_ref[5:6] * two).astype(BF16)


def block_forward(h, own, other, mod, weights):
    count, rows = own.shape[0], 256
    row = lambda width: pl.BlockSpec((rows, width), lambda i: (i, 0))
    sds = jax.ShapeDtypeStruct
    return pl.pallas_call(
        block_kernel,
        grid=(count // rows,),
        in_specs=[
            row(D),
            row(D),
            pl.BlockSpec((count, 3 * D), lambda i: (0, 0)),
            pl.BlockSpec((count, 3 * D), lambda i: (0, 0)),
            pl.BlockSpec((8, D), lambda i: (0, 0)),
            pl.BlockSpec((4, D, 3 * D), lambda i: (0, 0, 0)),
        ],
        out_specs=[row(D), row(D), row(128), row(D), row(D), row(D), row(FF), row(FF), row(D)],
        out_shape=[
            sds((count, D), BF16),
            sds((count, D), BF16),
            sds((count, 128), F32),
            sds((count, D), F32),
            sds((count, D), F32),
            sds((count, D), BF16),
            sds((count, FF), F32),
            sds((count, FF), BF16),
            sds((count, D), F32),
        ],
        compiler_params=params(),
        cost_estimate=cost(8e9, 1.2e7, 3e6),
        name="block_forward",
    )(h, own, own, other, mod, weights)


def head_kernel(h_ref, truth_ref, w_ref, fwd_ref, back_ref, dh_ref, g_ref, loss_ref, *, seed):
    count = h_ref.shape[0]
    x, inverse = normal(h_ref[...].astype(F32))
    flat = x.astype(BF16)
    pred = [dot(flat, w_ref[j]) for j in range(4)]
    pred = [jnp.concatenate(pred[:2], axis=-1), jnp.concatenate(pred[2:], axis=-1)]
    row = lax.broadcasted_iota(jnp.int32, (D, 256), 0)
    col = lax.broadcasted_iota(jnp.int32, (D, 256), 1)
    inside = col < PIXELS // 2
    true = []
    for b in range(2):
        pick = jnp.logical_and(row == 2 * col + b, inside).astype(BF16)
        true.append(dot(truth_ref[...], pick).astype(BF16))
    fwd = parts(fwd_ref[...], 2)
    back = parts(back_ref[...], 2)
    entries = LATP * CHANNELS * 2 * LONP
    loss = jnp.zeros((1, 1), F32)
    grads = [[], []]
    for p in range(count // LONP):
        part = slice(p * LONP, (p + 1) * LONP)
        seen = parts(jnp.concatenate([pred[0][part], pred[1][part]], axis=0), 2)
        waves = dot(fwd[0], seen[0]) + (dot(fwd[0], seen[1]) + dot(fwd[1], seen[0]))
        want = jnp.concatenate([true[0][part], true[1][part]], axis=0)
        target = dot(fwd[0], want) + dot(fwd[1], want)
        top, low = waves[:LONP], waves[LONP:]
        gap = (top * top + low * low) - (
            target[:LONP] * target[:LONP] + target[LONP:] * target[LONP:]
        )
        loss = loss + jnp.sum(gap * gap, axis=(0, 1), keepdims=True)
        scaled = gap * (4.0 * seed / entries)
        d_waves = parts(jnp.concatenate([scaled * top, scaled * low], axis=0), 2)
        d_seen = dot(back[0], d_waves[0]) + (dot(back[0], d_waves[1]) + dot(back[1], d_waves[0]))
        d_seen = d_seen.astype(BF16)
        grads[0].append(d_seen[:LONP])
        grads[1].append(d_seen[LONP:])
    loss_ref[...] = jnp.broadcast_to(loss * (seed / entries), loss_ref.shape)
    d_flat = jnp.zeros((count, D), F32)
    for b in range(2):
        whole = jnp.concatenate(grads[b], axis=0)
        for j in range(2):
            piece = whole[:, 128 * j : 128 * (j + 1)]
            d_flat = d_flat + dot_nt(piece, w_ref[2 * b + j])
            g_ref[2 * b + j] = dot_tn(flat, piece).astype(BF16)
    dh_ref[...] = normal_back(d_flat, x, inverse).astype(BF16)


def head(h, data, weights, basis_fwd, basis_back, seed, tokens):
    count = h.shape[0]
    sds = jax.ShapeDtypeStruct
    whole = lambda shape: pl.BlockSpec(shape, lambda i: (0,) * len(shape))
    return pl.pallas_call(
        lambda *refs: head_kernel(*refs, seed=seed),
        grid=(1,),
        in_specs=[
            whole((count, D)),
            pl.BlockSpec((count, D), lambda i: (tokens // count, 0)),
            pl.BlockSpec((4, D, 128), lambda i: (0, 0, 3 * D // 128)),
            whole((256, 256)),
            whole((256, 256)),
        ],
        out_specs=[whole((count, D)), whole((4, D, 128)), whole((8, 128))],
        out_shape=[sds((count, D), BF16), sds((4, D, 128), BF16), sds((8, 128), F32)],
        compiler_params=params(),
        cost_estimate=cost(3e9, 3e6),
        name="head",
    )(h, data, weights, basis_fwd, basis_back)


def gelu_slope(u):
    k = math.sqrt(2.0 / math.pi)
    t = jnp.tanh(k * (u + 0.044715 * (u * u * u)))
    return 0.5 * (1.0 + t) + 0.5 * u * (1.0 - t * t) * k * (1.0 + 3 * 0.044715 * (u * u))


def column_sum(v):
    return jnp.sum(v, axis=0, keepdims=True)


def mlp_back_kernel(
    dout_ref,
    two_ref,
    act_ref,
    units_ref,
    n2_ref,
    mid_ref,
    one_ref,
    att_ref,
    mod_ref,
    w_ref,
    dmid_ref,
    datt_ref,
    g_ref,
    gout_ref,
    dmod_ref,
):
    d_out = dout_ref[...].astype(F32)
    d_two = (mod_ref[5:6] * d_out).astype(BF16)
    g_gate_two = column_sum(d_out * two_ref[...])
    d_n2 = jnp.zeros(d_out.shape, F32)
    n2 = n2_ref[...]
    for j in range(2):
        part = slice(HALF * j, HALF * (j + 1))
        g_ref[2 + j] = dot_tn(d_two, act_ref[:, part]).astype(BF16)
        d_units = (gelu_slope(units_ref[:, part]) * dot(d_two, w_ref[2 + j, :, D:])).astype(BF16)
        g_ref[j] = dot_tn(n2, d_units).astype(BF16)
        d_n2 = d_n2 + dot_nt(d_units, w_ref[j, :, D:])
    x, inverse = normal(mid_ref[...])
    g_shift = column_sum(d_n2)
    g_scale = column_sum(d_n2 * x)
    d_mid = d_out + normal_back(d_n2 * (1.0 + mod_ref[4:5]), x, inverse)
    dmid_ref[...] = d_mid
    d_one = (mod_ref[2:3] * d_mid).astype(BF16)
    g_gate_one = column_sum(d_mid * one_ref[...])
    gout_ref[...] = dot_tn(att_ref[...], d_one).astype(BF16)
    datt_ref[...] = dot_nt(d_one, w_ref[3, :, :D]).astype(BF16)
    blank = jnp.zeros((2, D), F32)
    dmod_ref[...] = jnp.concatenate(
        [blank, g_gate_one, g_shift, g_scale, g_gate_two, blank], axis=0
    )


def mlp_back(d_out, saved, mod, weights):
    attended, lse, one, middle, n2, units, act, two = saved
    count = d_out.shape[0]
    sds = jax.ShapeDtypeStruct
    whole = lambda shape: pl.BlockSpec(shape, lambda i: (0,) * len(shape))
    return pl.pallas_call(
        mlp_back_kernel,
        grid=(1,),
        in_specs=[
            whole((count, D)),
            whole((count, D)),
            whole((count, FF)),
            whole((count, FF)),
            whole((count, D)),
            whole((count, D)),
            whole((count, D)),
            whole((count, D)),
            whole((8, D)),
            whole((4, D, 3 * D)),
        ],
        out_specs=[
            whole((count, D)),
            whole((count, D)),
            whole((4, D, HALF)),
            whole((D, D)),
            whole((8, D)),
        ],
        out_shape=[
            sds((count, D), F32),
            sds((count, D), BF16),
            sds((4, D, HALF), BF16),
            sds((D, D), BF16),
            sds((8, D), F32),
        ],
        compiler_params=params(56),
        cost_estimate=cost(6e9, 1.6e7, 1e6),
        name="mlp_back",
    )(d_out, two, act, units, n2, middle, one, attended, mod, weights)


def attention_back_kernel(q_ref, own_ref, other_ref, lse_ref, datt_ref, dq_ref, dk_ref, dv_ref):
    zero = jnp.zeros((), BF16)
    rows = q_ref.shape[0]
    first = pl.program_id(0) == 0
    for pair in range(HEADS // 2):
        a = 128 * pair
        here = slice(a, a + 128)
        q = q_ref[:, here]
        d_att = datt_ref[:, here]
        keys = jnp.concatenate([own_ref[:, D + a : D + a + 128], other_ref[:, D + a : D + a + 128]])
        vals = jnp.concatenate(
            [own_ref[:, 2 * D + a : 2 * D + a + 128], other_ref[:, 2 * D + a : 2 * D + a + 128]]
        )
        d_q = jnp.zeros((rows, 128), F32)
        d_k = jnp.zeros((keys.shape[0], 128), F32)
        d_v = jnp.zeros((keys.shape[0], 128), F32)
        for which, mask in enumerate(pair_masks()):
            head = 2 * pair + which
            k = jnp.where(mask, keys, zero)
            v = jnp.where(mask, vals, zero)
            scores = dot_nt(q * 0.125, k)
            probs = jnp.exp(scores - lse_ref[:, head : head + 1])
            d_probs = dot_nt(d_att, v)
            inner = jnp.sum(d_probs * probs, axis=-1, keepdims=True)
            d_scores = (probs * (d_probs - inner)).astype(BF16)
            d_q = d_q + dot(d_scores, k)
            d_k = d_k + dot_tn(d_scores, jnp.where(mask, q, zero))
            d_v = d_v + dot_tn(probs.astype(BF16), jnp.where(mask, d_att, zero))
        dq_ref[:, here] = (d_q * 0.125).astype(BF16)

        @pl.when(first)
        def _():
            dk_ref[:, here] = d_k * 0.125
            dv_ref[:, here] = d_v

        @pl.when(jnp.logical_not(first))
        def _():
            dk_ref[:, here] += d_k * 0.125
            dv_ref[:, here] += d_v


def attention_back(own, other, lse, d_att):
    count, rows = own.shape[0], 256
    sds = jax.ShapeDtypeStruct
    return pl.pallas_call(
        attention_back_kernel,
        grid=(count // rows,),
        in_specs=[
            pl.BlockSpec((rows, D), lambda i: (i, 0)),
            pl.BlockSpec((count, 3 * D), lambda i: (0, 0)),
            pl.BlockSpec((count, 3 * D), lambda i: (0, 0)),
            pl.BlockSpec((rows, 128), lambda i: (i, 0)),
            pl.BlockSpec((rows, D), lambda i: (i, 0)),
        ],
        out_specs=[
            pl.BlockSpec((rows, D), lambda i: (i, 0)),
            pl.BlockSpec((2 * count, D), lambda i: (0, 0)),
            pl.BlockSpec((2 * count, D), lambda i: (0, 0)),
        ],
        out_shape=[
            sds((count, D), BF16),
            sds((2 * count, D), F32),
            sds((2 * count, D), F32),
        ],
        compiler_params=params(),
        cost_estimate=cost(8e9, 8e6, 3e6),
        name="attention_back",
    )(own, own, other, lse, d_att)


def qkv_back_kernel(
    dq_ref, dk_ref, dv_ref, got_ref, normed_ref, h_ref, dmid_ref, gout_ref, mod_ref, w_ref,
    dh_ref, g_ref, dmod_ref,
):
    normed = normed_ref[...]
    d_k = (dk_ref[...] + got_ref[0]).astype(BF16)
    d_v = (dv_ref[...] + got_ref[1]).astype(BF16)
    d_n = jnp.zeros(normed.shape, F32)
    for j, piece in enumerate((dq_ref[...], d_k, d_v)):
        g_ref[j] = dot_tn(normed, piece).astype(BF16)
        d_n = d_n + dot_nt(piece, w_ref[j])
    g_ref[3] = gout_ref[...]
    x, inverse = normal(h_ref[...].astype(F32))
    g_shift = column_sum(d_n)
    g_scale = column_sum(d_n * x)
    dh_ref[...] = (
        dmid_ref[...] + normal_back(d_n * (1.0 + mod_ref[1:2]), x, inverse)
    ).astype(BF16)
    dmod_ref[...] = jnp.concatenate([g_shift, g_scale, jnp.zeros((6, D), F32)], axis=0)


def qkv_back(d_q, d_k, d_v, got, normed, h, d_mid, g_out, mod, weights):
    count = d_q.shape[0]
    sds = jax.ShapeDtypeStruct
    whole = lambda shape: pl.BlockSpec(shape, lambda i: (0,) * len(shape))
    return pl.pallas_call(
        qkv_back_kernel,
        grid=(1,),
        in_specs=[
            whole((count, D)),
            whole((count, D)),
            whole((count, D)),
            whole((2, count, D)),
            whole((count, D)),
            whole((count, D)),
            whole((count, D)),
            whole((D, D)),
            whole((8, D)),
            whole((4, D, D)),
        ],
        out_specs=[whole((count, D)), whole((4, D, D)), whole((8, D))],
        out_shape=[sds((count, D), BF16), sds((4, D, D), BF16), sds((8, D), F32)],
        compiler_params=params(),
        cost_estimate=cost(2e9, 8e6),
        name="qkv_back",
    )(d_q, d_k, d_v, got, normed, h, d_mid, g_out, mod, weights)


def swap(x, axis, size, by):
    return lax.ppermute(x, axis, [(i, i ^ by) for i in range(size)])


def place_kernel(where_ref, *refs, columns, rows):
    out_ref, sems = refs[-2], refs[-1]
    inputs = refs[:-2]
    s, z, c = where_ref[0], where_ref[1], where_ref[2]
    copies = []
    index = 0
    for jc in range(2):
        for js in range(columns):
            source = inputs[jc * columns + js]
            for jz in range(source.shape[0]):
                row = ((z ^ jz) * 2 + (c ^ jc)) * rows
                at = pl.ds(pl.multiple_of(row, rows), rows)
                target = out_ref.at[s ^ js, at] if columns > 1 else out_ref.at[at]
                copies.append(pltpu.make_async_copy(source.at[jz], target, sems.at[index]))
                index += 1
    for copy in copies:
        copy.start()
    for copy in copies:
        copy.wait()


def placed(where, own, got):
    columns, (zs, rows, width) = len(own), own[0].shape
    full = (zs * 2 * rows, width)
    shape = (columns,) + full if columns > 1 else full
    return pl.pallas_call(
        lambda *refs: place_kernel(*refs, columns=columns, rows=rows),
        in_specs=[pl.BlockSpec(memory_space=pltpu.SMEM)]
        + [pl.BlockSpec(memory_space=pl.ANY)] * (2 * columns),
        out_specs=pl.BlockSpec(memory_space=pl.ANY),
        out_shape=jax.ShapeDtypeStruct(shape, BF16),
        scratch_shapes=[pltpu.SemaphoreType.DMA((2 * columns * zs,))],
        cost_estimate=cost(0, 4 * math.prod(shape)),
        name="placed",
    )(where, *own, *got)


class Plain:
    def __init__(self, sizes):
        self.sizes = sizes

    def rows(self, x):
        return lax.all_gather(x, ("z", "c"), axis=0, tiled=True)

    def columns(self, x):
        return lax.all_gather(x, ("z", "c"), axis=1, tiled=True)

    def total(self, x, axes):
        return lax.psum(x, axes)

    def reduced(self, g):
        own = lax.psum_scatter(g.astype(F32), ("z", "c"), scatter_dimension=1, tiled=True)
        return lax.psum(own, "s")


class Squares(Plain):
    def __init__(self, sizes):
        super().__init__(sizes)
        self.s = lax.axis_index("s")
        self.z = lax.axis_index("z")
        self.c = lax.axis_index("c")
        self.where = jnp.stack([self.s, self.z, self.c]).astype(jnp.int32)

    def across(self, x, axis):
        return [swap(x, axis, 4, by) for by in (1, 2, 3)]

    def rows(self, x):
        own = jnp.stack([x] + self.across(x, "z"))
        return placed(self.where, [own], [swap(own, "c", 2, 1)])

    def columns(self, x):
        mine = lax.dynamic_index_in_dim(x, self.s, 0, keepdims=False)
        stack = jnp.stack([mine] + self.across(mine, "z"))
        own = [stack] + self.across(stack, "s")
        got = swap(jnp.stack(own), "c", 2, 1)
        return placed(self.where, own, [got[j] for j in range(4)])

    def total(self, x, axes):
        for axis in ("c", "s", "z"):
            if axis not in axes:
                continue
            if axis == "c":
                x = x + swap(x, "c", 2, 1)
            else:
                one, two, three = self.across(x, axis)
                x = (x + one) + (two + three)
        return x

    def scattered(self, x, axis, at):
        kept = lax.dynamic_index_in_dim(x, at, 0, keepdims=False).astype(F32)
        for by in (1, 2, 3):
            sent = lax.dynamic_index_in_dim(x, at ^ by, 0, keepdims=False)
            kept = kept + swap(sent, axis, 4, by).astype(F32)
        return kept.astype(BF16)

    def reduced(self, g):
        width = g.shape[-1]
        split = g.reshape(4, 4, 2, g.shape[1] // 8, width)
        kept = lax.dynamic_index_in_dim(split, self.c, 2, keepdims=False)
        sent = lax.dynamic_index_in_dim(split, 1 - self.c, 2, keepdims=False)
        x = (kept.astype(F32) + swap(sent, "c", 2, 1).astype(F32)).astype(BF16)
        x = self.scattered(x, "s", self.s)
        x = self.scattered(x, "z", self.z)
        one, two, three = self.across(x, "s")
        odd, high = self.s % 2 == 1, self.s >= 2
        pairs = [jnp.where(odd, b, a) for a, b in ((x, one), (one, x), (two, three), (three, two))]
        order = [jnp.where(high, pairs[i ^ 2], pairs[i]) for i in range(4)]
        return jnp.stack(order).astype(F32)


def layer_bundle(qkv, out, up, down_t, extra):
    pieces = []
    for j in range(4):
        first = qkv[:, D * j : D * (j + 1)] if j < 3 else out
        source = up if j < 2 else down_t
        second = source[:, HALF * (j % 2) : HALF * (j % 2 + 1)]
        row = [first, second] + ([extra[j]] if extra is not None else [])
        pieces.append(jnp.concatenate(row, axis=-1))
    return jnp.stack(pieces)


def per_device(sizes, *arrays):
    (tiles_in, truth_in, labels, var_ids, basis) = arrays[:5]
    masters, moments, averages = arrays[5:12], arrays[12:19], arrays[19:26]
    embed_w, qkv_w, out_w, up_w, down_w, ada_w, head_w = masters
    segments, dp = sizes["s"], sizes["z"] * 2
    micro, tokens = tiles_in.shape[0], tiles_in.shape[1]
    half = tokens // 2
    assert segments == 2 * micro
    rows = D // dp
    move = Squares(sizes) if segments == 4 and sizes["z"] == 4 else Plain(sizes)
    s, c = lax.axis_index("s"), lax.axis_index("c")

    emb_t = jnp.pad(embed_w.astype(BF16).T, ((0, 0), (0, ECOLS - EROWS)))
    down_t = down_w.astype(BF16).transpose(0, 2, 1)
    head_b = head_w.astype(BF16).reshape(rows, PIXELS // 2, 2)
    head_b = jnp.pad(head_b, ((0, 0), (0, 256 - PIXELS // 2), (0, 0)))
    head_b = [head_b[:, 128 * (j % 2) : 128 * (j % 2) + 128, j // 2] for j in range(4)]
    qkv_b, out_b, up_b = qkv_w.astype(BF16), out_w.astype(BF16), up_w.astype(BF16)
    bundles = [
        layer_bundle(qkv_b[l], out_b[l], up_b[l], down_t[l], head_b if l == 1 else None)
        for l in range(LAYERS)
    ]

    which = s % micro
    tiles = lax.dynamic_index_in_dim(tiles_in, which, 0, keepdims=False)
    truth = lax.dynamic_index_in_dim(truth_in, which, 0, keepdims=False)
    label = lax.dynamic_index_in_dim(labels, which, 0, keepdims=False)

    def seen_from(core):
        first = lax.dynamic_slice_in_dim(tiles, core * half, half)
        second = lax.dynamic_slice_in_dim(tiles, (1 - core) * half, half)
        third = lax.dynamic_slice_in_dim(truth, core * half, half)
        x = jnp.concatenate([first, second, third])
        x = jnp.pad(x, ((0, 0), (0, D - PIXELS)))
        lane = lax.broadcasted_iota(jnp.int32, x.shape, 1)
        return jnp.where(lane == LABEL_LANE, label.astype(BF16), x)

    pairs = []
    for a in range(segments):
        for b in range(sizes["z"]):
            base = (a * sizes["z"] + b) * 2
            pairs.append((base + a // micro, base + 1 - a // micro))
    sent = lax.ppermute(seen_from(1 - c), CHIP, pairs)
    data = jnp.where(c == s // micro, seen_from(c), sent)
    label = data[0, LABEL_LANE].astype(jnp.int32)

    emb = move.rows(emb_t)

    lead = embed_w[LEAD:].astype(BF16).astype(F32)
    ada = ada_w.astype(BF16).astype(F32)
    silu = jax.nn.silu(lead)
    mods = jnp.einsum("gd,ldm->lgm", silu, ada, precision=lax.Precision.HIGHEST)
    mods = jnp.pad(mods.reshape(LAYERS * GROUPS, 6 * D), ((0, 2), (0, 0)))
    mods = move.total(mods, ("z", "c"))

    def modulation(layer):
        row = lax.dynamic_index_in_dim(mods, layer * GROUPS + label, 0, keepdims=False)
        return jnp.pad(row.reshape(6, D), ((0, 2), (0, 0)))

    weights = [move.columns(b) for b in bundles]

    vid4 = jnp.pad(jnp.repeat(var_ids, 4), (0, D - PIXELS), constant_values=-1)[None].astype(
        jnp.int32
    )
    h0, agg = embed(data, emb, vid4, tokens)

    def forward(h, h_own, oth, oth_start, layer):
        mod = modulation(layer)
        normed, own = qkv_rows(h, 0, half, mod, weights[layer])
        _, other = qkv_rows(oth, oth_start, half, mod, weights[layer])
        out, *saved = block_forward(h, own, other, mod, weights[layer])
        return out, (mod, normed, own, other, saved)

    h1, kept0 = forward(h0, h0, h0, half, 0)
    h1_other = swap(h1, "c", 2, 1)
    h2, kept1 = forward(h1, h1, h1_other, 0, 1)

    forecasts = micro * dp
    by_column = basis.reshape(LONP, 2, 2 * LONP).transpose(1, 0, 2).reshape(2 * LONP, 2 * LONP)
    d_h2, g_head, loss = head(h2, data, weights[1], by_column.T, by_column, 1.0 / forecasts, tokens)

    def backward(d_out, h, kept, layer):
        mod, normed, own, other, saved = kept
        d_mid, d_att, g_ff, g_out, dmod = mlp_back(d_out, saved, mod, weights[layer])
        d_q, d_k, d_v = attention_back(own, other, saved[1], d_att)
        got = swap(jnp.stack([d_k[half:], d_v[half:]]), "c", 2, 1)
        d_h, g_att, dmod_one = qkv_back(
            d_q, d_k, d_v, got, normed, h, d_mid, g_out, mod, weights[layer]
        )
        return d_h, g_ff, g_att, (dmod + dmod_one)[:6].reshape(6 * D)

    d_h1, g_ff1, g_att1, dmod1 = backward(d_h2, h1, kept1, 1)
    got_ff1 = move.reduced(jnp.concatenate([g_ff1, g_head], axis=-1))
    got_att1 = move.reduced(g_att1)
    d_h0, g_ff0, g_att0, dmod0 = backward(d_h1, h0, kept0, 0)
    got_ff0 = move.reduced(g_ff0)
    g_emb = embed_back(d_h0, data, agg, emb, vid4)
    got_att0 = move.reduced(jnp.concatenate([g_att0, g_emb], axis=-1))

    hot = (jnp.arange(GROUPS) == label).astype(F32)[:, None]
    sums = jnp.concatenate([hot * dmod0[None], hot * dmod1[None]])
    sums = jnp.concatenate([sums, jnp.broadcast_to(loss[:1, :1], (2, 6 * D))])
    sums = move.total(sums, ("s", "z", "c"))
    loss_value = sums[LAYERS * GROUPS, 0]
    by_lead = sums[: LAYERS * GROUPS].reshape(LAYERS, GROUPS, 6 * D)
    highest = lax.Precision.HIGHEST
    g_ada = jnp.einsum("gd,lgm->ldm", silu, by_lead, precision=highest)
    d_silu = jnp.einsum("ldm,lgm->gd", ada, by_lead, precision=highest)
    gate = jax.nn.sigmoid(lead)
    g_lead = d_silu * (gate * (1.0 + lead * (1.0 - gate)))

    ff = [got_ff0[..., :HALF], got_ff1[..., :HALF]]
    att = [got_att0[..., :D], got_att1]
    spread = lambda x: x.transpose(1, 0, 2).reshape(rows, -1)
    g_qkv = jnp.stack([spread(x[:3]) for x in att])
    g_out = jnp.stack([x[3] for x in att])
    g_up = jnp.stack([spread(x[:2]) for x in ff])
    g_down = jnp.stack([spread(x[2:]).T for x in ff])
    g_embed = spread(got_att0[..., D:]).T[:EROWS]
    g_embed = jnp.concatenate([g_embed[:LEAD], g_lead])
    g_hw = got_ff1[..., HALF:].reshape(2, 2, rows, 128).transpose(2, 1, 3, 0)
    g_hw = g_hw.reshape(rows, 256, 2)[:, : PIXELS // 2].reshape(rows, PIXELS)
    grads = (g_embed, g_qkv, g_out, g_up, g_down, g_ada, g_hw)

    squares = sum(jnp.sum(g * g) for g in grads)
    squares = move.total(jnp.full((8, 128), squares, F32), ("z", "c"))[0, 0]
    norm = jnp.sqrt(squares)
    factor = CLIP / jnp.maximum(norm, CLIP)
    count = sum(w.size for w in masters) * dp
    rate = 0.02 * math.sqrt(count) / CLIP
    new_w, new_m, new_a = [], [], []
    for i, (w, m, a, g) in enumerate(zip(masters, moments, averages, grads)):
        g = g * factor
        m = KEEP * m + g
        w = w - rate * (BOOST if i == 0 else 1.0) * (g + KEEP * m)
        new_w.append(w)
        new_m.append(m)
        new_a.append(KEEP * a + (1.0 - KEEP) * w)
    return (loss_value, norm, *new_w, *new_m, *new_a)


def solution(mesh):
    segments, dp = mesh.shape["segment"], mesh.shape["dp"]
    sizes = {"s": segments, "z": dp // 2, "c": 2}
    split = Mesh(mesh.devices.reshape(segments, dp // 2, 2), CHIP)
    d = ("z", "c")
    weights = (
        P(None, d),
        P(None, d, None),
        P(None, d, None),
        P(None, d, None),
        P(None, None, d),
        P(None, d, None),
        P(d, None),
    )
    return jax.shard_map(
        lambda *arrays: per_device(sizes, *arrays),
        mesh=split,
        in_specs=(P(d, None, None), P(d, None, None), P(d), P(), P()) + weights * 3,
        out_specs=(P(), P()) + weights * 3,
        check_vma=False,
    )
```

time: 1680 us -> 664 us (0.40)
  waiting for transfers between devices: 1130 us -> 57.8 us
  Pallas kernels: 0 us -> 343 us
  starting transfers between devices: 192 us -> 93.4 us
  blocking collectives: 85.9 us -> 0 us
  loops' own time: 49.1 us -> 0 us
  matrix products: 37.2 us -> 4.59 us
    ppermute x10 -> x77, waiting for transfers between devices: 679 us -> 57.8 us  [the longest x76 57.8 us: swap(): return lax.ppermute(x, axis, [(i, i ^ by) for i in range(size)])]
    pallas_call x0 -> x18, Pallas kernels: none -> 343 us  [the longest x3 244 us: placed(): pl.pallas_call(lambda *refs: place_kernel(*refs, columns=columns, rows=ro...]
    reduce_scatter x7 -> x0, waiting for transfers between devices: 304 us -> none  [the longest x1 77.9 us: per_device(): lax.psum_scatter(stacked[4], 'dp', scatter_dimension=1, tiled=True)]
    ppermute x10 -> x77, starting transfers between devices: 191 us -> 93.4 us  [the longest x76 90.9 us: swap(): return lax.ppermute(x, axis, [(i, i ^ by) for i in range(size)])]
    all_gather x4 -> x0, waiting for transfers between devices: 81.6 us -> none  [the longest x1 40.3 us: per_device(): lax.all_gather(halves[5], 'dp', axis=1, tiled=True)]
    psum x1 -> x0, waiting for transfers between devices: 63.7 us -> none  [per_device(): lax.psum((shards[0], shards[1], shards[2], shards[3], shards[4], shards[5...]
    another operation x12 -> x0, loops' own time: 49.1 us -> none  [the longest x1 19.4 us: per_device(): lax.fori_loop(0, micro_count + segment_count - 1, forward_tick, (jnp.zero...]
    all_gather x3 -> x0, blocking collectives: 49 us -> none  [the longest x1 17.3 us: per_device(): lax.all_gather(halves[2], 'dp', axis=1, tiled=True)]
  transfers between devices with their start and end apart: 22 -> 77, of which waited for: 21 -> 31; matrix products, arithmetic and copies ran while one was open for 3% -> 12% of each run, Pallas kernels for 0% -> 46%
where the time goes in v1:
time: 664 us; the launch traced here: 655 us
  Pallas kernels  343 us (52%)
  starting transfers between devices  93.4 us (14%)
  local copies, waits for them, and re-layouts  91.2 us (14%)
  waiting for transfers between devices  57.8 us (9%)
  other arithmetic  53.8 us (8%)
  between operations  10.8 us (2%)
    pallas_call x3, Pallas kernels, placed(): pl.pallas_call(lambda *refs: place_kernel(*refs, columns=columns, rows=ro...  244 us
    ppermute x76, starting transfers between devices, swap(): return lax.ppermute(x, axis, [(i, i ^ by) for i in range(size)])  90.9 us
    ppermute x76, waiting for transfers between devices, swap(): return lax.ppermute(x, axis, [(i, i ^ by) for i in range(size)])  57.8 us
    unnamed x276, local copies, waits for them, and re-layouts  50 us
    pallas_call x2, Pallas kernels, attention_back(): pl.pallas_call(attention_back_kernel, grid=(count // rows,), in_specs=[pl...  26.5 us
    pallas_call x2, Pallas kernels, block_forward(): pl.pallas_call(block_kernel, grid=(count // rows,), in_specs=[row(D), row...  25.1 us
    pallas_call x2, Pallas kernels, mlp_back(): pl.pallas_call(mlp_back_kernel, grid=(1,), in_specs=[whole((count, D)), w...  22.1 us
  transfers between devices with their start and end apart: 77, of which 31 were waited for; matrix products, arithmetic and copies ran while one was open for 12% of the time, Pallas kernels for 46%

profile of v1, /device:TPU:0, one launch (start us, length us, event | category | flops | bytes accessed | tf_op | source)
XLA Modules:
  0.0 654.9 jit_solution(17368947192777877296)
XLA Ops:
  2.3 5.0 collective-permute-start.3
  12.7 3.8 collective-permute-start.11
  16.6 6.2 constant_dynamic-slice_fusion.3
  36.0 3.8 collective-permute-start.18
  59.2 6.8 %collective-permute-done.13.refs_3_ = bf16[4,48,1152]{2,1,0:T(8,128)(2,1)S(1)} collective-permute-done((bf16[4,48,1152]{2,1,0:T(8,128)(2,1)S(1)}, bf16[4,48,1152]{2,1,0:T(8,128)(2,1)S(1)}, u32[]{:S(2)}, u32[]{:S(2)}) %collective-permute-start.13) | collective-permute-done | bytes 442400 | tf_op jit(solution)/shard_map/ppermute | solution.py:619
  66.0 3.6 collective-permute-start.8
  76.2 13.8 %placed.3.emb_ref = bf16[384,512]{1,0:T(8,128)(2,1)} custom-call(s32[3]{0:T(128)} %pad_add_fusion.refs_0_, bf16[4,48,512]{2,1,0:T(8,128)(2,1)} %copy-done.101, bf16[4,48,512]{2,1,0:T(8,128)(2,1)} %copy-done.122), custom_call_target="tpu_custom_call" | custom-call | bytes 786432 | tf_op jit(solution)/shard_map/placed/pallas_call | solution.py:647
  90.0 3.7 collective-permute-done.20.refs_3_
  98.8 5.4 embed.1
  104.3 3.5 slice_bitcast_fusion.8
  107.8 109.3 %placed.4.w_ref = bf16[4,384,1152]{2,1,0:T(8,128)(2,1)} custom-call(s32[3]{0:T(128)} %pad_add_fusion.refs_0_, bf16[4,48,1152]{2,1,0:T(8,128)(2,1)} %copy-done.91, bf16[4,48,1152]{2,1,0:T(8,128)(2,1)} %copy-done.88, bf16[4,48,1152]{2,1,0:T(8,128)(2,1)} %copy-done.89, bf16[4,48,1152]{2,1,0:T(8,128)(2,1)} %copy-done.90, ...), custom_call_target="tpu_custom_call" | custom-call | bytes 7077888 | tf_op jit(solution)/shard_map/placed/pallas_call | solution.py:647
  223.2 12.4 %block_forward.2 = (bf16[512,384]{1,0:T(8,128)(2,1)S(1)}, bf16[512,384]{1,0:T(8,128)(2,1)S(1)}, f32[512,128]{1,0:T(8,128)S(1)}, f32[512,384]{1,0:T(8,128)S(1)}, ...) custom-call(bf16[1024,384]{1,0:T(8,128)(2,1)S(1)} %get-tuple-element, ...), custom_call_target="tpu_custom_call" | custom-call | flops 8000000000 | bytes 12000000 | tf_op jit(solution)/shard_map/block_forward/pallas_call | solution.py:310
  245.3 121.2 %placed.5.w_ref.refs_2_ = bf16[4,384,1280]{2,1,0:T(8,128)(2,1)} custom-call(s32[3]{0:T(128)} %pad_add_fusion.refs_0_, bf16[4,48,1280]{2,1,0:T(8,128)(2,1)} %copy-done.84, bf16[4,48,1280]{2,1,0:T(8,128)(2,1)} %copy-done.85, bf16[4,48,1280]{2,1,0:T(8,128)(2,1)} %copy-done.86, bf16[4,48,1280]{2,1,0:T(8,128)(2,1)} %copy-done.87, ...), custom_call_target="tpu_custom_call" | custom-call | bytes 7864320 | tf_op jit(solution)/shard_map/placed/pallas_call | solution.py:647
  372.6 12.7 %block_forward.3 = (bf16[512,384]{1,0:T(8,128)(2,1)S(1)}, bf16[512,384]{1,0:T(8,128)(2,1)S(1)}, f32[512,128]{1,0:T(8,128)S(1)}, f32[512,384]{1,0:T(8,128)S(1)}, ...) custom-call(bf16[512,384]{1,0:T(8,128)(2,1)S(1)} %get-tuple-element., ...), custom_call_target="tpu_custom_call" | custom-call | flops 8000000000 | bytes 12000000 | tf_op jit(solution)/shard_map/block_forward/pallas_call | solution.py:310
  387.7 4.0 head.1
  392.5 11.1 %mlp_back.2 = (f32[512,384]{1,0:T(8,128)}, bf16[512,384]{1,0:T(8,128)(2,1)}, bf16[4,384,768]{2,1,0:T(8,128)(2,1)}, bf16[384,384]{1,0:T(8,128)(2,1)}, f32[8,384]{1,0:T(8,128)}) custom-call(bf16[512,384]{1,0:T(8,128)(2,1)} %copy-done.52, f32[512,384]{1,0:T(8,128)} %copy-done.56, bf16[512,1536]{1,0:T(8,128)(2,1)} %copy-done.51, f32[512,1536]{1,0:T(8,128)} %copy-done.47, ...), custom_call_target="tpu_custom_call" | custom-call | flops 6000000000 | bytes 16000000 | tf_op jit(solution)/shard_map/mlp_back/pallas_call | solution.py:465
  404.6 13.3 %attention_back.2 = (bf16[512,384]{1,0:T(8,128)(2,1)S(1)}, f32[1024,384]{1,0:T(8,128)S(1)}, f32[1024,384]{1,0:T(8,128)S(1)}) custom-call(bf16[512,1152]{1,0:T(8,128)(2,1)S(1)} %copy-done.41, bf16[512,1152]{1,0:T(8,128)(2,1)S(1)} %copy-done.41, bf16[512,1152]{1,0:T(8,128)(2,1)S(1)} %copy-done.43, f32[512,128]{1,0:T(8,128)S(1)} %get-tuple-element.80.lse_ref, ...), custom_call_target="tpu_custom_call" | custom-call | flops 8000000000 | bytes 8000000 | tf_op jit(solution)/shard_map/attention_back/pallas_call | solution.py:544
  438.4 11.0 %mlp_back.3 = (f32[512,384]{1,0:T(8,128)}, bf16[512,384]{1,0:T(8,128)(2,1)}, bf16[4,384,768]{2,1,0:T(8,128)(2,1)}, bf16[384,384]{1,0:T(8,128)(2,1)}, f32[8,384]{1,0:T(8,128)}) custom-call(bf16[512,384]{1,0:T(8,128)(2,1)} %copy-done.46, f32[512,384]{1,0:T(8,128)} %copy-done.59, bf16[512,1536]{1,0:T(8,128)(2,1)} %copy-done.53, f32[512,1536]{1,0:T(8,128)} %copy-done.50, ...), custom_call_target="tpu_custom_call" | custom-call | flops 6000000000 | bytes 16000000 | tf_op jit(solution)/shard_map/mlp_back/pallas_call | solution.py:465
  450.5 13.2 %attention_back.3 = (bf16[512,384]{1,0:T(8,128)(2,1)S(1)}, f32[1024,384]{1,0:T(8,128)S(1)}, f32[1024,384]{1,0:T(8,128)S(1)}) custom-call(bf16[512,1152]{1,0:T(8,128)(2,1)S(1)} %copy-done.37, bf16[512,1152]{1,0:T(8,128)(2,1)S(1)} %copy-done.37, bf16[512,1152]{1,0:T(8,128)(2,1)S(1)} %copy-done.39, f32[512,128]{1,0:T(8,128)S(1)} %copy-done.67, ...), custom_call_target="tpu_custom_call" | custom-call | flops 8000000000 | bytes 8000000 | tf_op jit(solution)/shard_map/attention_back/pallas_call | solution.py:544
  491.9 4.1 collective-permute-done.46
  522.3 4.6 collective-permute-done.56
  526.9 3.9 collective-permute-done.55
  553.7 3.3 qkv_back.3
  588.6 4.6 collective-permute-done.36
  (584 shorter events, 259.6 us)
Async XLA Ops:
  2.3 33.1 %collective-permute-start.3 = (bf16[48,512]{1,0:T(8,128)(2,1)}, bf16[48,512]{1,0:T(8,128)(2,1)}, u32[]{:S(2)}, u32[]{:S(2)}) collective-permute-start(bf16[48,512]{1,0:T(8,128)(2,1)} %get-tuple-element.281), channel_id=1, source_target_pairs={{0,6},{2,4},{4,2},{6,0},{1,7},{3,5},{5,3},{7,1},{8,14},{10,12},{12... | collective-permute-start | bytes 147464 | tf_op jit(solution)/shard_map/ppermute | solution.py:619
  7.4 28.7 %collective-permute-start.2 = (bf16[48,512]{1,0:T(8,128)(2,1)}, bf16[48,512]{1,0:T(8,128)(2,1)}, u32[]{:S(2)}, u32[]{:S(2)}) collective-permute-start(bf16[48,512]{1,0:T(8,128)(2,1)} %get-tuple-element.281), channel_id=1, source_target_pairs={{0,4},{2,6},{4,0},{6,2},{1,5},{3,7},{5,1},{7,3},{8,12},{10,14},{12... | collective-permute-start | bytes 147464 | tf_op jit(solution)/shard_map/ppermute | solution.py:619
  7.4 32.5 %collective-permute-start.1 = (bf16[48,512]{1,0:T(8,128)(2,1)}, bf16[48,512]{1,0:T(8,128)(2,1)}, u32[]{:S(2)}, u32[]{:S(2)}) collective-permute-start(bf16[48,512]{1,0:T(8,128)(2,1)} %get-tuple-element.281), channel_id=1, source_target_pairs={{0,2},{2,0},{4,6},{6,4},{1,3},{3,1},{5,7},{7,5},{8,10},{10,8},{12,... | collective-permute-start | bytes 147464 | tf_op jit(solution)/shard_map/ppermute | solution.py:619
  12.7 28.0 %collective-permute-start.11 = (bf16[48,1152]{1,0:T(8,128)(2,1)}, bf16[48,1152]{1,0:T(8,128)(2,1)}, u32[]{:S(2)}, u32[]{:S(2)}) collective-permute-start(bf16[48,1152]{1,0:T(8,128)(2,1)} %bitcast.26), channel_id=1, source_target_pairs={{0,6},{2,4},{4,2},{6,0},{1,7},{3,5},{5,3},{7,1},{8,14},{10,12},{12... | collective-permute-start | bytes 331784 | tf_op jit(solution)/shard_map/ppermute | solution.py:619
  16.6 24.9 %collective-permute-start.10 = (bf16[48,1152]{1,0:T(8,128)(2,1)}, bf16[48,1152]{1,0:T(8,128)(2,1)}, u32[]{:S(2)}, u32[]{:S(2)}) collective-permute-start(bf16[48,1152]{1,0:T(8,128)(2,1)} %bitcast.26), channel_id=1, source_target_pairs={{0,4},{2,6},{4,0},{6,2},{1,5},{3,7},{5,1},{7,3},{8,12},{10,14},{12... | collective-permute-start | bytes 331784 | tf_op jit(solution)/shard_map/ppermute | solution.py:619
  44.4 21.6 %collective-permute-start.13 = (bf16[4,48,1152]{2,1,0:T(8,128)(2,1)S(1)}, bf16[4,48,1152]{2,1,0:T(8,128)(2,1)S(1)}, u32[]{:S(2)}, u32[]{:S(2)}) collective-permute-start(bf16[4,48,1152]{2,1,0:T(8,128)(2,1)S(1)} %get-tuple-element.224.refs_1_), channel_id=1, source_target_pairs={{0,16},{8,24},{16,0},{24,8},{1,17},{9,25},{17,1},{25,9},{2,18},{10... | collective-permute-start | bytes 1327112 | tf_op jit(solution)/shard_map/ppermute | solution.py:619
  46.6 23.0 %collective-permute-start.14 = (bf16[4,48,1152]{2,1,0:T(8,128)(2,1)S(1)}, bf16[4,48,1152]{2,1,0:T(8,128)(2,1)S(1)}, u32[]{:S(2)}, u32[]{:S(2)}) collective-permute-start(bf16[4,48,1152]{2,1,0:T(8,128)(2,1)S(1)} %get-tuple-element.224.refs_1_), channel_id=1, source_target_pairs={{0,24},{8,16},{16,8},{24,0},{1,25},{9,17},{17,9},{25,1},{2,26},{10... | collective-permute-start | bytes 1327112 | tf_op jit(solution)/shard_map/ppermute | solution.py:619
  49.4 47.4 %collective-permute-start = (bf16[1536,384]{1,0:T(8,128)(2,1)}, bf16[1536,384]{1,0:T(8,128)(2,1)}, u32[]{:S(2)}, u32[]{:S(2)}) collective-permute-start(bf16[1536,384]{1,0:T(8,128)(2,1)} %fusion.15), channel_id=1, source_target_pairs={{0,1},{2,3},{4,5},{6,7},{8,9},{10,11},{12,13},{14,15},{17,16},{19,... | collective-permute-start | bytes 3538952 | tf_op jit(solution)/shard_map/ppermute | solution.py:785
  52.0 23.6 %collective-permute-start.4 = (bf16[4,48,512]{2,1,0:T(8,128)(2,1)S(1)}, bf16[4,48,512]{2,1,0:T(8,128)(2,1)S(1)}, u32[]{:S(2)}, u32[]{:S(2)}) collective-permute-start(bf16[4,48,512]{2,1,0:T(8,128)(2,1)S(1)} %pad_maximum_fusion.9.refs_1_), channel_id=1, source_target_pairs={{0,1},{1,0},{2,3},{3,2},{4,5},{5,4},{6,7},{7,6},{8,9},{9,8},{10,11... | collective-permute-start | bytes 589832 | tf_op jit(solution)/shard_map/ppermute | solution.py:619
  55.9 15.4 %collective-permute-start.7 = (f32[8,2304]{1,0:T(8,128)S(1)}, f32[8,2304]{1,0:T(8,128)S(1)}, u32[]{:S(2)}, u32[]{:S(2)}) collective-permute-start(f32[8,2304]{1,0:T(8,128)S(1)} %pad_add_fusion.1), channel_id=1, source_target_pairs={{0,4},{2,6},{4,0},{6,2},{1,5},{3,7},{5,1},{7,3},{8,12},{10,14},{12... | collective-permute-start | bytes 221192 | tf_op jit(solution)/shard_map/ppermute | solution.py:619
  71.3 18.7 %collective-permute-start.19 = (bf16[4,48,1280]{2,1,0:T(8,128)(2,1)S(1)}, bf16[4,48,1280]{2,1,0:T(8,128)(2,1)S(1)}, u32[]{:S(2)}, u32[]{:S(2)}) collective-permute-start(bf16[4,48,1280]{2,1,0:T(8,128)(2,1)S(1)} %get-tuple-element.222.refs_1_), channel_id=1, source_target_pairs={{0,8},{8,0},{16,24},{24,16},{1,9},{9,1},{17,25},{25,17},{2,10},{10... | collective-permute-start | bytes 1474568 | tf_op jit(solution)/shard_map/ppermute | solution.py:619
  72.2 21.5 %collective-permute-start.20 = (bf16[4,48,1280]{2,1,0:T(8,128)(2,1)S(1)}, bf16[4,48,1280]{2,1,0:T(8,128)(2,1)S(1)}, u32[]{:S(2)}, u32[]{:S(2)}) collective-permute-start(bf16[4,48,1280]{2,1,0:T(8,128)(2,1)S(1)} %get-tuple-element.222.refs_1_), channel_id=1, source_target_pairs={{0,16},{8,24},{16,0},{24,8},{1,17},{9,25},{17,1},{25,9},{2,18},{10... | collective-permute-start | bytes 1474568 | tf_op jit(solution)/shard_map/ppermute | solution.py:619
  74.1 19.7 %collective-permute-start.21 = (bf16[4,48,1280]{2,1,0:T(8,128)(2,1)S(1)}, bf16[4,48,1280]{2,1,0:T(8,128)(2,1)S(1)}, u32[]{:S(2)}, u32[]{:S(2)}) collective-permute-start(bf16[4,48,1280]{2,1,0:T(8,128)(2,1)S(1)} %get-tuple-element.222.refs_1_), channel_id=1, source_target_pairs={{0,24},{8,16},{16,8},{24,0},{1,25},{9,17},{17,9},{25,1},{2,26},{10... | collective-permute-start | bytes 1474568 | tf_op jit(solution)/shard_map/ppermute | solution.py:619
  75.6 28.7 %collective-permute-start.15 = (bf16[4,4,48,1152]{3,2,1,0:T(8,128)(2,1)}, bf16[4,4,48,1152]{3,2,1,0:T(8,128)(2,1)}, u32[]{:S(2)}, u32[]{:S(2)}) collective-permute-start(bf16[4,4,48,1152]{3,2,1,0:T(8,128)(2,1)} %pad_maximum_fusion.2), channel_id=1, source_target_pairs={{0,1},{1,0},{2,3},{3,2},{4,5},{5,4},{6,7},{7,6},{8,9},{9,8},{10,11... | collective-permute-start | bytes 5308424 | tf_op jit(solution)/shard_map/ppermute | solution.py:619
  96.7 145.8 %collective-permute-start.22 = (bf16[4,4,48,1280]{3,2,1,0:T(8,128)(2,1)}, bf16[4,4,48,1280]{3,2,1,0:T(8,128)(2,1)}, u32[]{:S(2)}, u32[]{:S(2)}) collective-permute-start(bf16[4,4,48,1280]{3,2,1,0:T(8,128)(2,1)} %pad_maximum_fusion.1), channel_id=1, source_target_pairs={{0,1},{1,0},{2,3},{3,2},{4,5},{5,4},{6,7},{7,6},{8,9},{9,8},{10,11... | collective-permute-start | bytes 5898248 | tf_op jit(solution)/shard_map/ppermute | solution.py:619
  240.7 129.5 %collective-permute-start.23 = (bf16[512,384]{1,0:T(8,128)(2,1)S(1)}, bf16[512,384]{1,0:T(8,128)(2,1)S(1)}, u32[]{:S(2)}, u32[]{:S(2)}) collective-permute-start(bf16[512,384]{1,0:T(8,128)(2,1)S(1)} %get-tuple-element.77.h_ref), channel_id=1, source_target_pairs={{0,1},{1,0},{2,3},{3,2},{4,5},{5,4},{6,7},{7,6},{8,9},{9,8},{10,11... | collective-permute-start | bytes 1179656 | tf_op jit(solution)/shard_map/ppermute | solution.py:619
  429.7 38.4 %collective-permute-start.66 = (bf16[4,48,896]{2,1,0:T(8,128)(2,1)}, bf16[4,48,896]{2,1,0:T(8,128)(2,1)}, u32[]{:S(2)}, u32[]{:S(2)}) collective-permute-start(bf16[4,48,896]{2,1,0:T(8,128)(2,1)} %get-tuple-element.202), channel_id=1, source_target_pairs={{0,24},{8,16},{16,8},{24,0},{1,25},{9,17},{17,9},{25,1},{2,26},{10... | collective-permute-start | bytes 1032200 | tf_op jit(solution)/shard_map/ppermute | solution.py:619
  430.5 37.6 %collective-permute-start.65 = (bf16[4,48,896]{2,1,0:T(8,128)(2,1)}, bf16[4,48,896]{2,1,0:T(8,128)(2,1)}, u32[]{:S(2)}, u32[]{:S(2)}) collective-permute-start(bf16[4,48,896]{2,1,0:T(8,128)(2,1)} %get-tuple-element.203), channel_id=1, source_target_pairs={{0,16},{8,24},{16,0},{24,8},{1,17},{9,25},{17,1},{25,9},{2,18},{10... | collective-permute-start | bytes 1032200 | tf_op jit(solution)/shard_map/ppermute | solution.py:619
  431.5 36.6 %collective-permute-start.64 = (bf16[4,48,896]{2,1,0:T(8,128)(2,1)}, bf16[4,48,896]{2,1,0:T(8,128)(2,1)}, u32[]{:S(2)}, u32[]{:S(2)}) collective-permute-start(bf16[4,48,896]{2,1,0:T(8,128)(2,1)} %get-tuple-element.201), channel_id=1, source_target_pairs={{0,8},{8,0},{16,24},{24,16},{1,9},{9,1},{17,25},{25,17},{2,10},{10... | collective-permute-start | bytes 1032200 | tf_op jit(solution)/shard_map/ppermute | solution.py:619
  467.4 78.2 %collective-permute-start.25 = (f32[2,512,384]{2,1,0:T(8,128)}, f32[2,512,384]{2,1,0:T(8,128)}, u32[]{:S(2)}, u32[]{:S(2)}) collective-permute-start(f32[2,512,384]{2,1,0:T(8,128)} %pad_maximum_fusion.4), channel_id=1, source_target_pairs={{0,1},{1,0},{2,3},{3,2},{4,5},{5,4},{6,7},{7,6},{8,9},{9,8},{10,11... | collective-permute-start | bytes 4718600 | tf_op jit(solution)/shard_map/ppermute | solution.py:619
  485.9 27.2 %collective-permute-start.53 = (bf16[4,4,48,768]{3,2,1,0:T(8,128)(2,1)}, bf16[4,4,48,768]{3,2,1,0:T(8,128)(2,1)}, u32[]{:S(2)}, u32[]{:S(2)}) collective-permute-start(bf16[4,4,48,768]{3,2,1,0:T(8,128)(2,1)} %dynamic-slice_bitcast_fusion.1), channel_id=1, source_target_pairs={{0,1},{1,0},{2,3},{3,2},{4,5},{5,4},{6,7},{7,6},{8,9},{9,8},{10,11... | collective-permute-start | bytes 3538952 | tf_op jit(solution)/shard_map/ppermute | solution.py:619
  542.1 27.7 %collective-permute-start.60 = (bf16[48,768]{1,0:T(8,128)(2,1)}, bf16[48,768]{1,0:T(8,128)(2,1)}, u32[]{:S(2)}, u32[]{:S(2)}) collective-permute-start(bf16[48,768]{1,0:T(8,128)(2,1)} %fusion.39), channel_id=1, source_target_pairs={{0,24},{8,16},{16,8},{24,0},{1,25},{9,17},{17,9},{25,1},{2,26},{10... | collective-permute-start | bytes 221192 | tf_op jit(solution)/shard_map/ppermute | solution.py:619
  543.4 26.4 %collective-permute-start.61 = (bf16[48,768]{1,0:T(8,128)(2,1)}, bf16[48,768]{1,0:T(8,128)(2,1)}, u32[]{:S(2)}, u32[]{:S(2)}) collective-permute-start(bf16[48,768]{1,0:T(8,128)(2,1)} %fusion.39), channel_id=1, source_target_pairs={{0,16},{8,24},{16,0},{24,8},{1,17},{9,25},{17,1},{25,9},{2,18},{10... | collective-permute-start | bytes 221192 | tf_op jit(solution)/shard_map/ppermute | solution.py:619
  544.0 25.8 %collective-permute-start.62 = (bf16[48,768]{1,0:T(8,128)(2,1)}, bf16[48,768]{1,0:T(8,128)(2,1)}, u32[]{:S(2)}, u32[]{:S(2)}) collective-permute-start(bf16[48,768]{1,0:T(8,128)(2,1)} %fusion.39), channel_id=1, source_target_pairs={{0,8},{8,0},{16,24},{24,16},{1,9},{9,1},{17,25},{25,17},{2,10},{10... | collective-permute-start | bytes 221192 | tf_op jit(solution)/shard_map/ppermute | solution.py:619
  (186 other events, 1890.1 us)
